TPU v7x, 128 devices: a whole 4x4x4 slice. The times are simulated.
128 devices in a mesh: pairs: 128 (over z, x, y, core).
Axes of the slice: x: 4, y: 4, z: 4, core: 2. Of those that a mesh axis runs over, the one named last changes fastest.
Arguments:
- pno_basis: bfloat16 [1024, 192, 128], P('pairs'), may hold values from -0.4375 to 0.4375
- pno_count: int32 [1024], P('pairs'), may hold values from 64 to 128
- partner_owner: int32 [1024, 12], P('pairs'), may hold values from 0 to 127, all different within a row; in each aligned block of 8 rows (0 to 7, 8 to 15, ...) at most 2 rows name the same one
- partner_local: int32 [1024, 12], P('pairs'), may hold values from 0 to 7
- exchange_k: bfloat16 [1024, 128, 128], P('pairs'), may hold values from -6 to 6
- ladder_factor: bfloat16 [1024, 40, 128, 128], P('pairs'), may hold values from -0.15625 to 0.15625
- pno_energy: float32 [1024, 128], P('pairs'), may hold values from 0.3 to 3
- occ_energy: float32 [1024], P('pairs'), may hold values from -2 to -0.6
- coupling_fock: bfloat16 [1024, 12], P('pairs'), may hold values from -3 to 3
Outputs:
- amplitudes: float32 [1024, 128, 128], P('pairs')
Inputs may be any that keep to these rules, and one draw needn't show every extreme that they name: `partner_owner`: the 12 partners of one pair have different owners. Among the 8 pairs of one device no device is named more than 2 times, and in some devices' pairs one device is named exactly 2 times. Partner c of pair p is the pair numbered partner_owner[p, c] * 8 + partner_local[p, c]. Pair p uses its first pno_count[p] orbitals; the others are padding.
All inputs are finite; a program needn't handle non-finite values.
Results may differ from a plain program's by a relative error of at most 0.009.
Values may be sent and summed in bfloat16 or wider, within the bound.
No kernel may reach another device: no remote copies, remote signals or barrier semaphores. Data moves between devices by JAX's collectives and lax.ppermute only.
A program may use at most 128 MiB of HBM per device.

v0:
```python
import jax
import jax.numpy as jnp
from jax import lax
from jax.sharding import PartitionSpec as P

ITERS = 3


level_shift = 0.3


def gather_rows(source_rows, chosen, usable):
    picked = source_rows[jnp.clip(chosen, 0, source_rows.shape[0] - 1)]
    extended = usable.reshape(usable.shape + (1,) * (picked.ndim - usable.ndim))
    return jnp.where(extended, picked, jnp.zeros_like(picked))


def shards(
    pno_basis,
    pno_count,
    partner_owner,
    partner_local,
    exchange_k,
    ladder_factor,
    pno_energy,
    occ_energy,
    coupling_fock,
):
    peer_count = lax.axis_size("pairs")
    own_pairs, domain, orbitals = pno_basis.shape
    fitted = ladder_factor.shape[1]
    partners = partner_owner.shape[1]
    listed = own_pairs * partners
    slot_count = max(2, (listed + peer_count - 1) // peer_count)
    columns = lax.broadcasted_iota(jnp.int32, (own_pairs, orbitals), 1)
    live_cols = (columns < pno_count[:, None]).astype(jnp.float32)
    masked_basis = pno_basis * live_cols[:, None, :].astype(jnp.bfloat16)
    flat_owner = partner_owner.reshape(listed)
    flat_local = partner_local.reshape(listed)
    owner_onehot = (
        flat_owner[:, None] == lax.broadcasted_iota(jnp.int32, (listed, peer_count), 1)
    ).astype(jnp.int32)
    before = jnp.cumsum(owner_onehot, axis=0) - owner_onehot
    slot_rank = jnp.sum(before * owner_onehot, axis=1)
    flat_slot = flat_owner * slot_count + slot_rank
    slot_onehot = (
        slot_rank[:, None] == lax.broadcasted_iota(jnp.int32, (listed, slot_count), 1)
    ).astype(jnp.int32)
    labelled = slot_onehot * (flat_local + 1)[:, None]
    wanted = jnp.sum(owner_onehot[:, :, None] * labelled[:, None, :], axis=0) - 1
    asked_rows = lax.all_to_all(wanted, "pairs", split_axis=0, concat_axis=0, tiled=True)
    asked_usable = asked_rows >= 0
    sent_basis = gather_rows(masked_basis, asked_rows, asked_usable)
    arrived_basis = lax.all_to_all(sent_basis, "pairs", split_axis=0, concat_axis=0, tiled=True)
    partner_basis = arrived_basis.reshape(peer_count * slot_count, domain, orbitals)[flat_slot]
    partner_basis = partner_basis.reshape(own_pairs, partners, domain, orbitals)
    margin = jnp.einsum(
        "rva,rcvb->rcab", masked_basis, partner_basis, preferred_element_type=jnp.float32
    ).astype(jnp.bfloat16)
    energy_sum = pno_energy[:, :, None] + pno_energy[:, None, :] - occ_energy[:, None, None]
    divisor = energy_sum + level_shift
    driving = exchange_k.astype(jnp.float32) * (live_cols[:, :, None] * live_cols[:, None, :])
    amplitudes = -driving / divisor
    weights = coupling_fock.astype(jnp.float32)
    group_width = 8
    for iteration in range(ITERS):
        sent_amps = amplitudes.astype(jnp.bfloat16)
        sent_rows = gather_rows(sent_amps, asked_rows, asked_usable)
        arrived_amps = lax.all_to_all(sent_rows, "pairs", split_axis=0, concat_axis=0, tiled=True)

        def add_group(group_index, total):
            factors = lax.dynamic_slice_in_dim(
                ladder_factor, group_index * group_width, group_width, 1
            )
            ladder_half = jnp.einsum(
                "rqac,rcd->rqad", factors, sent_amps, preferred_element_type=jnp.float32
            ).astype(jnp.bfloat16)
            return total + jnp.einsum(
                "rqad,rqbd->rab", ladder_half, factors, preferred_element_type=jnp.float32
            )

        ladder = lax.fori_loop(
            0,
            fitted // group_width,
            add_group,
            jnp.zeros((own_pairs, orbitals, orbitals), jnp.float32),
        )
        partner_amps = arrived_amps.reshape(peer_count * slot_count, orbitals, orbitals)[flat_slot]
        partner_amps = partner_amps.reshape(own_pairs, partners, orbitals, orbitals)
        left_half = jnp.einsum(
            "rcab,rcbd->rcad", margin, partner_amps, preferred_element_type=jnp.float32
        )
        left_half = (left_half * weights[:, :, None, None]).astype(jnp.bfloat16)
        gathered_terms = jnp.einsum(
            "rcad,rced->rcae", left_half, margin, preferred_element_type=jnp.float32
        ).astype(jnp.bfloat16)
        coupled = jnp.sum(gathered_terms, axis=1, dtype=jnp.float32)
        residual = driving + energy_sum * amplitudes + coupled + ladder
        amplitudes = amplitudes - residual / divisor
    return amplitudes


def solution(mesh):
    return jax.shard_map(
        shards,
        mesh=mesh,
        in_specs=(
            P("pairs", None, None),
            P("pairs"),
            P("pairs", None),
            P("pairs", None),
            P("pairs", None, None),
            P("pairs", None, None, None),
            P("pairs", None),
            P("pairs"),
            P("pairs", None),
        ),
        out_specs=P("pairs", None, None),
        check_vma=False,
    )
```

profile of v0, /device:TPU:1, one launch (start us, length us, event | category | flops | bytes accessed | tf_op | source)
XLA Modules:
  0.0 601.0 jit_solution(8261185862522598821)
XLA Ops:
  2.8 11.5 %all-to-all-start = ((s32[128,1,2]{2,1,0:T(1,128)}), s32[128,1,2]{2,1,0:T(1,128)S(1)}, u32[]{:S(2)}, u32[]{:S(2)}) async-start(s32[128,1,2]{2,1,0:T(1,128)} %copy.19), calls=%async_computation | async-start | bytes 131072 | tf_op jit(solution)/shard_map/all_to_all | solution.py:51
  16.4 7.5 %all-to-all-done = s32[128,1,2]{2,1,0:T(1,128)S(1)} async-done(((s32[128,1,2]{2,1,0:T(1,128)}), s32[128,1,2]{2,1,0:T(1,128)S(1)}, u32[]{:S(2)}, u32[]{:S(2)}) %all-to-all-start) | async-done | bytes 1056 | tf_op jit(solution)/shard_map/all_to_all | solution.py:51
  24.5 8.5 %gather_fusion.2 = bf16[256,128,128]{2,1,0:T(8,128)(2,1)} fusion(bf16[8,128,128]{2,1,0:T(8,128)(2,1)S(1)} %fusion.87, s32[1024]{0:T(1024)S(1)} %pad_clamp_fusion.1), kind=kCustom, calls=%fused_computation.2 | custom fusion | bytes 16778240 | tf_op jit(solution)/shard_map/gather | solution.py:13
  33.0 7.2 %broadcast_select_fusion.3 = bf16[128,2,128,128]{3,2,1,0:T(8,128)(2,1)} fusion(bf16[128,2,128,128]{3,2,1,0:T(8,128)(2,1)} %bitcast.86, pred[128,2]{1,0:T(8,128)(4,1)S(1)} %copy.21), kind=kLoop, calls=%fused_computation.35 | loop fusion | flops 4194304 | bytes 16777472 | tf_op jit(solution)/shard_map/jit(_where)/select_n | solution.py:15
  45.7 10.4 %gather_fusion = bf16[256,192,128]{2,1,0:T(8,128)(2,1)} fusion(bf16[8,192,128]{2,1,0:T(8,128)(2,1)S(1)} %broadcast_multiply_fusion, s32[1024]{0:T(1024)S(1)} %pad_clamp_fusion.1), kind=kCustom, calls=%fused_computation | custom fusion | bytes 25166848 | tf_op jit(solution)/shard_map/gather | solution.py:13
  56.1 10.8 %broadcast_select_fusion = bf16[128,2,192,128]{3,2,1,0:T(8,128)(2,1)} fusion(bf16[128,2,192,128]{3,2,1,0:T(8,128)(2,1)} %bitcast.84, pred[128,2]{1,0:T(8,128)(4,1)S(1)} %copy.21), kind=kLoop, calls=%fused_computation.32 | loop fusion | flops 6291456 | bytes 25166080 | tf_op jit(solution)/shard_map/jit(_where)/select_n | solution.py:15
  66.9 76.9 %all-to-all-done.2 = bf16[128,2,128,128]{3,2,1,0:T(8,128)(2,1)} async-done(((bf16[128,2,128,128]{3,2,1,0:T(8,128)(2,1)}), bf16[128,2,128,128]{3,2,1,0:T(8,128)(2,1)}, u32[]{:S(2)}, u32[]{:S(2)}) %all-to-all-start.2) | async-done | bytes 8388640 | tf_op jit(solution)/shard_map/all_to_all | solution.py:69
  143.8 10.2 %all-to-all-start.1 = ((bf16[128,2,192,128]{3,2,1,0:T(8,128)(2,1)}), bf16[128,2,192,128]{3,2,1,0:T(8,128)(2,1)}, u32[]{:S(2)}, u32[]{:S(2)}) async-start(bf16[128,2,192,128]{3,2,1,0:T(8,128)(2,1)} %broadcast_select_fusion), calls=%async_computation.1 | async-start | bytes 25165824 | tf_op jit(solution)/shard_map/all_to_all | solution.py:54
  154.1 18.4 %while.42 = (s32[]{:T(128)}, f32[8,128,128]{2,1,0:T(8,128)S(1)}, bf16[8,40,128,128]{3,2,1,0:T(8,128)(2,1)}, bf16[8,128,128]{2,1,0:T(8,128)(2,1)S(1)}, s32[]{:T(128)}, /*index=5*/s32[]{:T(128)}, s32[]{:T(128)}, s32[]{:T(128)}) while((s32[]{:T(128)}, f32[8,128,128]{2,1,0:T(8,128)S(1)}, bf16[8,40,128,128]{3,2,1,0:T(8,128)(2,1)}, ...), condition=%wide.region_5.6_spmd.clone, body=%wide.region_4.5_spmd.clone.sunk | while | flops 538181632 | bytes 5506700 | solution.py:82
  178.6 129.5 %all-to-all-done.1 = bf16[128,2,192,128]{3,2,1,0:T(8,128)(2,1)} async-done(((bf16[128,2,192,128]{3,2,1,0:T(8,128)(2,1)}), bf16[128,2,192,128]{3,2,1,0:T(8,128)(2,1)}, u32[]{:S(2)}, u32[]{:S(2)}) %all-to-all-start.1) | async-done | bytes 12582944 | tf_op jit(solution)/shard_map/all_to_all | solution.py:54
  308.1 8.0 %gather_fusion.1 = bf16[96,192,128]{2,1,0:T(8,128)(2,1)} fusion(bf16[256,192,128]{2,1,0:T(8,128)(2,1)} %bitcast.4, s32[1024]{0:T(1024)S(1)} %pad_clamp_fusion), kind=kCustom, calls=%fused_computation.1 | custom fusion | bytes 9437568 | tf_op jit(solution)/shard_map/gather | solution.py:55
  316.1 6.1 %convolution_convert_fusion = bf16[8,12,128,128]{3,2,1,0:T(8,128)(2,1)} fusion(bf16[8,12,192,128]{3,2,1,0:T(8,128)(2,1)} %bitcast.88, bf16[8,192,128]{2,1,0:T(8,128)(2,1)S(1)} %broadcast_multiply_fusion), kind=kOutput, calls=%fused_computation.51 | convolution fusion | flops 605552640 | bytes 8257536 | tf_op jit(solution)/shard_map/rva,rcvb->rcab/dot_general | solution.py:57
  328.6 8.5 %gather_fusion.4 = bf16[256,128,128]{2,1,0:T(8,128)(2,1)} fusion(bf16[8,128,128]{2,1,0:T(8,128)(2,1)S(1)} %get-tuple-element.422, s32[1024]{0:T(1024)S(1)} %pad_clamp_fusion.1), kind=kCustom, calls=%fused_computation.4 | custom fusion | bytes 16778240 | tf_op jit(solution)/shard_map/gather | solution.py:13
  337.2 7.3 %broadcast_select_fusion.2 = bf16[128,2,128,128]{3,2,1,0:T(8,128)(2,1)} fusion(bf16[128,2,128,128]{3,2,1,0:T(8,128)(2,1)} %bitcast.87, pred[128,2]{1,0:T(8,128)(4,1)S(1)} %copy.21), kind=kLoop, calls=%fused_computation.34 | loop fusion | flops 4194304 | bytes 16777472 | tf_op jit(solution)/shard_map/jit(_where)/select_n | solution.py:15
  344.4 8.9 %all-to-all-start.3 = ((bf16[128,2,128,128]{3,2,1,0:T(8,128)(2,1)}), bf16[128,2,128,128]{3,2,1,0:T(8,128)(2,1)}, u32[]{:S(2)}, u32[]{:S(2)}) async-start(bf16[128,2,128,128]{3,2,1,0:T(8,128)(2,1)} %broadcast_select_fusion.2), calls=%async_computation.3 | async-start | bytes 16777216 | tf_op jit(solution)/shard_map/all_to_all | solution.py:69
  353.3 18.4 %while.43 = (s32[]{:T(128)}, f32[8,128,128]{2,1,0:T(8,128)S(1)}, bf16[8,40,128,128]{3,2,1,0:T(8,128)(2,1)}, bf16[8,128,128]{2,1,0:T(8,128)(2,1)S(1)}, s32[]{:T(128)}, /*index=5*/s32[]{:T(128)}, s32[]{:T(128)}, s32[]{:T(128)}) while((s32[]{:T(128)}, f32[8,128,128]{2,1,0:T(8,128)S(1)}, bf16[8,40,128,128]{3,2,1,0:T(8,128)(2,1)}, ...), condition=%wide.region_8.9_spmd.clone, body=%wide.region_7.8_spmd.clone.sunk | while | flops 538181632 | bytes 5506700 | solution.py:82
  371.7 79.5 %all-to-all-done.3 = bf16[128,2,128,128]{3,2,1,0:T(8,128)(2,1)} async-done(((bf16[128,2,128,128]{3,2,1,0:T(8,128)(2,1)}), bf16[128,2,128,128]{3,2,1,0:T(8,128)(2,1)}, u32[]{:S(2)}, u32[]{:S(2)}) %all-to-all-start.3) | async-done | bytes 8388640 | tf_op jit(solution)/shard_map/all_to_all | solution.py:69
  451.3 6.2 %gather_fusion.5 = bf16[96,128,128]{2,1,0:T(8,128)(2,1)} fusion(bf16[256,128,128]{2,1,0:T(8,128)(2,1)} %bitcast.14, s32[1024]{0:T(1024)S(1)} %pad_clamp_fusion), kind=kCustom, calls=%fused_computation.5 | custom fusion | bytes 6291840 | tf_op jit(solution)/shard_map/gather | solution.py:88
  463.8 8.5 %gather_fusion.6 = bf16[256,128,128]{2,1,0:T(8,128)(2,1)} fusion(bf16[8,128,128]{2,1,0:T(8,128)(2,1)S(1)} %get-tuple-element.446, s32[1024]{0:T(1024)S(1)} %pad_clamp_fusion.1), kind=kCustom, calls=%fused_computation.6 | custom fusion | bytes 16778240 | tf_op jit(solution)/shard_map/gather | solution.py:13
  472.3 7.3 %broadcast_select_fusion.1 = bf16[128,2,128,128]{3,2,1,0:T(8,128)(2,1)} fusion(bf16[128,2,128,128]{3,2,1,0:T(8,128)(2,1)} %bitcast.85, pred[128,2]{1,0:T(8,128)(4,1)S(1)} %copy.21), kind=kLoop, calls=%fused_computation.33 | loop fusion | flops 4194304 | bytes 16777472 | tf_op jit(solution)/shard_map/jit(_where)/select_n | solution.py:15
  479.6 10.2 %all-to-all-start.4 = ((bf16[128,2,128,128]{3,2,1,0:T(8,128)(2,1)}), bf16[128,2,128,128]{3,2,1,0:T(8,128)(2,1)}, u32[]{:S(2)}, u32[]{:S(2)}) async-start(bf16[128,2,128,128]{3,2,1,0:T(8,128)(2,1)} %broadcast_select_fusion.1), calls=%async_computation.4 | async-start | bytes 16777216 | tf_op jit(solution)/shard_map/all_to_all | solution.py:69
  489.8 18.4 %while.44 = (s32[]{:T(128)}, f32[8,128,128]{2,1,0:T(8,128)S(1)}, bf16[8,40,128,128]{3,2,1,0:T(8,128)(2,1)}, bf16[8,128,128]{2,1,0:T(8,128)(2,1)S(1)}, s32[]{:T(128)}, /*index=5*/s32[]{:T(128)}, s32[]{:T(128)}, s32[]{:T(128)}) while((s32[]{:T(128)}, f32[8,128,128]{2,1,0:T(8,128)S(1)}, bf16[8,40,128,128]{3,2,1,0:T(8,128)(2,1)}, ...), condition=%wide.region_11.12_spmd.clone, body=%wide.region_10.11_spmd.clone.sunk | while | flops 538181632 | bytes 5506700 | solution.py:82
  508.2 79.5 %all-to-all-done.4 = bf16[128,2,128,128]{3,2,1,0:T(8,128)(2,1)} async-done(((bf16[128,2,128,128]{3,2,1,0:T(8,128)(2,1)}), bf16[128,2,128,128]{3,2,1,0:T(8,128)(2,1)}, u32[]{:S(2)}, u32[]{:S(2)}) %all-to-all-start.4) | async-done | bytes 8388640 | tf_op jit(solution)/shard_map/all_to_all | solution.py:69
  587.7 6.2 %gather_fusion.7 = bf16[96,128,128]{2,1,0:T(8,128)(2,1)} fusion(bf16[256,128,128]{2,1,0:T(8,128)(2,1)} %bitcast.17, s32[1024]{0:T(1024)S(1)} %pad_clamp_fusion), kind=kCustom, calls=%fused_computation.7 | custom fusion | bytes 6291840 | tf_op jit(solution)/shard_map/gather | solution.py:88
  (63 shorter events, 91.7 us)
Async XLA Ops:
  2.8 21.1 %all-to-all-start = ((s32[128,1,2]{2,1,0:T(1,128)}), s32[128,1,2]{2,1,0:T(1,128)S(1)}, u32[]{:S(2)}, u32[]{:S(2)}) async-start(s32[128,1,2]{2,1,0:T(1,128)} %copy.19), calls=%async_computation | async-start | bytes 131072 | tf_op jit(solution)/shard_map/all_to_all | solution.py:51
  40.3 5.4 copy-start.1
  40.3 103.5 %all-to-all-start.2 = ((bf16[128,2,128,128]{3,2,1,0:T(8,128)(2,1)}), bf16[128,2,128,128]{3,2,1,0:T(8,128)(2,1)}, u32[]{:S(2)}, u32[]{:S(2)}) async-start(bf16[128,2,128,128]{3,2,1,0:T(8,128)(2,1)} %broadcast_select_fusion.3), calls=%async_computation.2 | async-start | bytes 16777216 | tf_op jit(solution)/shard_map/all_to_all | solution.py:69
  66.9 87.2 %copy-start.3 = (s32[8,12]{1,0:T(8,128)S(1)}, s32[8,12]{1,0:T(8,128)}, u32[]{:S(2)}) copy-start(s32[8,12]{1,0:T(8,128)} %param.17) | copy-start | bytes 1156
  66.9 87.3 %copy-start.5 = (bf16[8,12]{1,0:T(8,128)(2,1)S(1)}, bf16[8,12]{1,0:T(8,128)(2,1)}, u32[]{:S(2)}) copy-start(bf16[8,12]{1,0:T(8,128)(2,1)} %param.23) | copy-start | bytes 580
  143.8 164.4 %all-to-all-start.1 = ((bf16[128,2,192,128]{3,2,1,0:T(8,128)(2,1)}), bf16[128,2,192,128]{3,2,1,0:T(8,128)(2,1)}, u32[]{:S(2)}, u32[]{:S(2)}) async-start(bf16[128,2,192,128]{3,2,1,0:T(8,128)(2,1)} %broadcast_select_fusion), calls=%async_computation.1 | async-start | bytes 25165824 | tf_op jit(solution)/shard_map/all_to_all | solution.py:54
  322.2 6.0 copy-start
  322.2 6.0 %copy-start.2 = (f32[8,128]{1,0:T(8,128)S(1)}, f32[8,128]{1,0:T(8,128)}, u32[]{:S(2)}) copy-start(f32[8,128]{1,0:T(8,128)} %param.21) | copy-start | bytes 12292
  322.2 6.0 %copy-start.4 = (f32[8]{0:T(128)S(1)}, f32[8]{0:T(128)}, u32[]{:S(2)}) copy-start(f32[8]{0:T(128)} %param.22) | copy-start | bytes 100
  344.4 106.8 %all-to-all-start.3 = ((bf16[128,2,128,128]{3,2,1,0:T(8,128)(2,1)}), bf16[128,2,128,128]{3,2,1,0:T(8,128)(2,1)}, u32[]{:S(2)}, u32[]{:S(2)}) async-start(bf16[128,2,128,128]{3,2,1,0:T(8,128)(2,1)} %broadcast_select_fusion.2), calls=%async_computation.3 | async-start | bytes 16777216 | tf_op jit(solution)/shard_map/all_to_all | solution.py:69
  479.6 108.2 %all-to-all-start.4 = ((bf16[128,2,128,128]{3,2,1,0:T(8,128)(2,1)}), bf16[128,2,128,128]{3,2,1,0:T(8,128)(2,1)}, u32[]{:S(2)}, u32[]{:S(2)}) async-start(bf16[128,2,128,128]{3,2,1,0:T(8,128)(2,1)} %broadcast_select_fusion.1), calls=%async_computation.4 | async-start | bytes 16777216 | tf_op jit(solution)/shard_map/all_to_all | solution.py:69
where the time goes:
time: 603 us; the launch traced here: 601 us
  waiting for transfers between devices  373 us (62%)
  matrix products  78.8 us (13%)
  local copies, waits for them, and re-layouts  64.4 us (11%)
  starting transfers between devices  46.2 us (8%)
  other arithmetic  37.9 us (6%)
    all_to_all x3, waiting for transfers between devices, shards(): lax.all_to_all(sent_rows, 'pairs', split_axis=0, concat_axis=0, tiled=True)  236 us
    all_to_all x1, waiting for transfers between devices, shards(): lax.all_to_all(sent_basis, 'pairs', split_axis=0, concat_axis=0, tiled=True)  129 us
    dot_general x15, matrix products, add_group(): jnp.einsum('rqad,rqbd->rab', ladder_half, factors, preferred_element_type...  54.8 us
    gather x4, local copies, waits for them, and re-layouts, gather_rows(): picked = source_rows[jnp.clip(chosen, 0, source_rows.shape[0] - 1)]  36 us
    select_n x4, other arithmetic, gather_rows(): return jnp.where(extended, picked, jnp.zeros_like(picked))  32.5 us
    all_to_all x3, starting transfers between devices, shards(): lax.all_to_all(sent_rows, 'pairs', split_axis=0, concat_axis=0, tiled=True)  24.4 us
    gather x3, local copies, waits for them, and re-layouts, shards(): arrived_amps.reshape(peer_count * slot_count, orbitals, orbitals)[flat_slot]  18.4 us
    dot_general x3, matrix products, shards(): jnp.einsum('rcad,rced->rcae', left_half, margin, preferred_element_type=j...  17.9 us
  transfers between devices with their start and end apart: 5, of which 5 were waited for; matrix products, arithmetic and copies ran while one was open for 14% of the time, Pallas kernels for 0%

commit v1 on v0

v1 whole, which is shorter than its diff:
```python
import functools

import jax
import jax.numpy as jnp
from jax import lax
from jax.experimental import pallas as pl
from jax.experimental.pallas import tpu as pltpu
from jax.sharding import PartitionSpec as P

ITERS = 3
LEVEL_SHIFT = 0.3
LANES = 128
F32 = jnp.float32
BF16 = jnp.bfloat16
NT = (((1,), (1,)), ((), ()))


def regroup(major, minor, turned):
    size = major * minor
    row = lax.broadcasted_iota(jnp.int32, (size, size), 0)
    col = lax.broadcasted_iota(jnp.int32, (size, size), 1)
    to, source = (col, row) if turned else (row, col)
    hit = source == lax.rem(to, major) * minor + lax.div(to, major)
    return jnp.where(hit, 1.0, 0.0).astype(BF16)


def side_by_side(matrix, chips):
    parts = matrix.shape[0] // chips
    return jnp.concatenate([matrix[i * chips : (i + 1) * chips] for i in range(parts)], axis=1)


def one_below_other(pieces):
    parts = pieces.shape[1] // LANES
    return jnp.concatenate([pieces[:, i * LANES : (i + 1) * LANES] for i in range(parts)], axis=0)


def store_pieces(stacked, send_ref, first_lane):
    chips, _, own, _ = send_ref.shape
    width = stacked.shape[1]
    back = regroup(chips, own, True)
    pieces = jnp.dot(back, stacked, preferred_element_type=F32).astype(BF16)
    pieces = pieces.reshape(chips, own, width)
    for core in range(2):
        send_ref[:, core, :, first_lane : first_lane + width] = pieces


def pack_kernel(sent_ref, basis_ref, asked_ref, send_ref):
    chips, _, own, width = send_ref.shape
    stacked = jnp.concatenate(
        [
            jnp.concatenate(
                [side_by_side(sent_ref[p], chips), side_by_side(basis_ref[p], chips)], axis=1
            )
            for p in range(own)
        ],
        axis=0,
    )
    store_pieces(stacked, send_ref, 0)
    send_ref[:, :, :, width - LANES :] = jnp.broadcast_to(
        asked_ref[...][None], (chips, 2, own, LANES)
    )


def pack(sent, masked_basis, asked, chips):
    own = sent.shape[0]
    width = (sent.shape[1] + masked_basis.shape[1]) // chips * LANES + LANES
    return pl.pallas_call(
        pack_kernel,
        out_shape=jax.ShapeDtypeStruct((chips, 2, own, width), BF16),
        name="pack",
    )(sent, masked_basis, asked)


def pick_kernel(list_ref, table_ref, out_ref, onehot_ref):
    half, group = list_ref.shape[1:]
    rows = table_ref.shape[0]
    lane = lax.broadcasted_iota(jnp.int32, (half, LANES), 1)
    for member in range(group):
        wanted = jnp.broadcast_to(list_ref[0, :, member : member + 1], (half, LANES))
        for tile in range(rows // LANES):
            hit = (wanted - tile * LANES) == lane
            onehot_ref[member * half : (member + 1) * half, tile * LANES : (tile + 1) * LANES] = (
                jnp.where(hit, 1.0, 0.0).astype(BF16)
            )
    picked = jnp.dot(onehot_ref[...], table_ref[...], preferred_element_type=F32)
    out_ref[...] = picked.astype(BF16).reshape(out_ref.shape)


def pick_pieces(lists, table, width):
    groups, half, group = lists.shape
    rows = table.shape[0]
    return pl.pallas_call(
        pick_kernel,
        grid=(groups,),
        in_specs=[
            pl.BlockSpec((1, half, group), lambda g: (g, 0, 0)),
            pl.BlockSpec((rows, width), lambda g: (0, 0)),
        ],
        out_specs=pl.BlockSpec((group, half, width), lambda g: (g, 0, 0)),
        out_shape=jax.ShapeDtypeStruct((groups * group, half, width), BF16),
        scratch_shapes=[pltpu.VMEM((group * half, rows), BF16)],
        cost_estimate=pl.CostEstimate(
            flops=2 * groups * group * half * rows * width,
            bytes_accessed=2 * (rows * width + groups * group * half * width),
            transcendentals=0,
        ),
        name="pick_pieces",
    )(lists, table)


def couple_kernel(first, last, *refs):
    refs = list(refs)
    weight_ref, arrived_ref = refs.pop(0), refs.pop(0)
    margin_in = refs.pop(0)
    amp_ref, rest_ref, div_ref = refs.pop(0), refs.pop(0), refs.pop(0)
    out_ref = refs.pop(0)
    sent_ref = send_ref = margin_out = None
    if not last:
        sent_ref, send_ref = refs.pop(0), refs.pop(0)
    if first:
        margin_out = refs.pop(0)
    total_ref, order_ref = refs
    step, steps = pl.program_id(0), pl.num_programs(0)
    chips, _, _, own, width = arrived_ref.shape

    @pl.when(step == 0)
    def _():
        total_ref[...] = jnp.zeros_like(total_ref)
        order_ref[...] = regroup(chips, own, False)

    for core in range(2):
        arrived = arrived_ref[:, core, 0].reshape(chips * own, width)
        ordered = jnp.dot(order_ref[...], arrived, preferred_element_type=F32).astype(BF16)
        for p in range(own):
            pieces = ordered[p * chips : (p + 1) * chips]
            amps = one_below_other(pieces[:, : 2 * LANES])
            if first:
                basis = one_below_other(pieces[:, 2 * LANES :])
                margin = jnp.dot(margin_in[p], basis, preferred_element_type=F32).astype(BF16)
                margin_out[0, core, p] = margin
            else:
                margin = margin_in[0, core, p]
            left = jnp.dot(margin, amps, preferred_element_type=F32)
            left = (left * weight_ref[p, core * steps + step]).astype(BF16)
            term = lax.dot_general(left, margin, NT, preferred_element_type=F32)
            total_ref[p] += term.astype(BF16).astype(F32)

    @pl.when(step == steps - 1)
    def _():
        for p in range(own):
            out_ref[p] = amp_ref[p] - (rest_ref[p] + total_ref[p]) / div_ref[p]
        if not last:
            sent_ref[...] = out_ref[...].astype(BF16)
            stacked = jnp.concatenate(
                [side_by_side(sent_ref[p], chips) for p in range(own)], axis=0
            )
            store_pieces(stacked, send_ref, 0)


def couple(first, last, weights, arrived, margin, amplitudes, rest, divisor):
    chips, _, steps, own, width = arrived.shape
    orbitals = amplitudes.shape[1]
    whole = pl.BlockSpec(amplitudes.shape, lambda c: (0, 0, 0))
    margin_spec = pl.BlockSpec((1, 2, own, orbitals, orbitals), lambda c: (c, 0, 0, 0, 0))
    margin_shape = jax.ShapeDtypeStruct((steps, 2, own, orbitals, orbitals), BF16)
    out_specs, out_shape = [whole], [jax.ShapeDtypeStruct(amplitudes.shape, F32)]
    if not last:
        send = (chips, 2, own, 2 * LANES)
        out_specs += [whole, pl.BlockSpec(send, lambda c: (0, 0, 0, 0))]
        out_shape += [
            jax.ShapeDtypeStruct(amplitudes.shape, BF16),
            jax.ShapeDtypeStruct(send, BF16),
        ]
    if first:
        out_specs.append(margin_spec)
        out_shape.append(margin_shape)
    return pl.pallas_call(
        functools.partial(couple_kernel, first, last),
        grid=(steps,),
        in_specs=[
            pl.BlockSpec(memory_space=pltpu.SMEM),
            pl.BlockSpec((chips, 2, 1, own, width), lambda c: (0, 0, c, 0, 0)),
            pl.BlockSpec(margin.shape, lambda c: (0, 0, 0)) if first else margin_spec,
            whole,
            whole,
            whole,
        ],
        out_specs=out_specs,
        out_shape=out_shape,
        scratch_shapes=[
            pltpu.VMEM(amplitudes.shape, F32),
            pltpu.VMEM((own * chips, own * chips), BF16),
        ],
        name="couple",
    )(weights, arrived, margin, amplitudes, rest, divisor)


def swap(values):
    return lax.all_to_all(values, "pairs", split_axis=0, concat_axis=0, tiled=True)


def shards(
    pno_basis,
    pno_count,
    partner_owner,
    partner_local,
    exchange_k,
    ladder_factor,
    pno_energy,
    occ_energy,
    coupling_fock,
):
    devices = lax.axis_size("pairs")
    chips = devices // 2
    own, domain, orbitals = pno_basis.shape
    fitted = ladder_factor.shape[1]
    partners = partner_owner.shape[1]
    half = own * partners // 2
    rows = devices * own
    group = 16
    columns = lax.broadcasted_iota(jnp.int32, (own, orbitals), 1)
    live_cols = (columns < pno_count[:, None]).astype(F32)
    masked_basis = pno_basis * live_cols[:, None, :].astype(BF16)
    energy_sum = pno_energy[:, :, None] + pno_energy[:, None, :] - occ_energy[:, None, None]
    divisor = energy_sum + LEVEL_SHIFT
    driving = exchange_k.astype(F32) * (live_cols[:, :, None] * live_cols[:, None, :])
    amplitudes = -driving / divisor
    weights = coupling_fock.astype(F32)

    asked = jnp.stack([partner_owner, partner_local], axis=0).astype(BF16)
    asked = asked.reshape(2, own, 2, partners // 2)
    asked = jnp.transpose(asked, (2, 0, 3, 1)).reshape(2, 2, half)
    asked = jnp.pad(asked, ((0, 0), (0, own - 2), (0, LANES - half)))

    def ladder_of(sent):
        group_width = 8

        def add_group(group_index, total):
            factors = lax.dynamic_slice_in_dim(
                ladder_factor, group_index * group_width, group_width, 1
            )
            ladder_half = jnp.einsum(
                "rqac,rcd->rqad", factors, sent, preferred_element_type=F32
            ).astype(BF16)
            return total + jnp.einsum(
                "rqad,rqbd->rab", ladder_half, factors, preferred_element_type=F32
            )

        return lax.fori_loop(
            0, fitted // group_width, add_group, jnp.zeros((own, orbitals, orbitals), F32)
        )

    sent = amplitudes.astype(BF16)
    send = pack(sent, masked_basis, asked, chips)
    margin = jnp.transpose(masked_basis, (0, 2, 1))
    lists = None
    for iteration in range(ITERS):
        first, last = iteration == 0, iteration == ITERS - 1
        held = swap(send.reshape(devices, own, send.shape[-1]))
        width = 2 * LANES
        if first:
            width = held.shape[-1] - LANES
            names = held[:, :2, width : width + half].astype(jnp.int32)
            lists = names[:, 0] * own + names[:, 1]
            lists = jnp.transpose(lists.reshape(devices // group, group, half), (0, 2, 1))
        arrived = swap(pick_pieces(lists, held.reshape(rows, held.shape[-1]), width))
        rest = driving + energy_sum * amplitudes + ladder_of(sent)
        results = couple(
            first,
            last,
            weights,
            arrived.reshape(chips, 2, partners // 2, own, width),
            margin,
            amplitudes,
            rest,
            divisor,
        )
        amplitudes = results[0]
        if not last:
            sent, send = results[1], results[2]
        if first:
            margin = results[3]
    return amplitudes


def solution(mesh):
    return jax.shard_map(
        shards,
        mesh=mesh,
        in_specs=(
            P("pairs", None, None),
            P("pairs"),
            P("pairs", None),
            P("pairs", None),
            P("pairs", None, None),
            P("pairs", None, None, None),
            P("pairs", None),
            P("pairs"),
            P("pairs", None),
        ),
        out_specs=P("pairs", None, None),
        check_vma=False,
    )
```

time: 603 us -> 380 us (0.63)
  waiting for transfers between devices: 373 us -> 105 us
  Pallas kernels: 0 us -> 101 us
  blocking collectives: 0 us -> 75.7 us
  local copies, waits for them, and re-layouts: 64.4 us -> 6.48 us
  starting transfers between devices: 46.2 us -> 15.2 us
  other arithmetic: 37.9 us -> 12.7 us
  matrix products: 78.8 us -> 62.7 us
    all_to_all x5 -> x3, waiting for transfers between devices: 373 us -> 105 us  [swap(): lax.all_to_all(values, 'pairs', split_axis=0, concat_axis=0, tiled=True)]
    pallas_call x0 -> x7, Pallas kernels: none -> 101 us  [the longest x3 64.9 us: couple(): pl.pallas_call(functools.partial(couple_kernel, first, last), grid=(steps...]
    all_to_all x0 -> x3, blocking collectives: none -> 75.7 us  [swap(): lax.all_to_all(values, 'pairs', split_axis=0, concat_axis=0, tiled=True)]
    gather x8 -> x0, local copies, waits for them, and re-layouts: 62.4 us -> none  [the longest x4 36 us: gather_rows(): picked = source_rows[jnp.clip(chosen, 0, source_rows.shape[0] - 1)]]
    select_n x6 -> x0, other arithmetic: 32.6 us -> none  [the longest x4 32.5 us: gather_rows(): return jnp.where(extended, picked, jnp.zeros_like(picked))]
    all_to_all x5 -> x3, starting transfers between devices: 46.2 us -> 15.2 us  [swap(): lax.all_to_all(values, 'pairs', split_axis=0, concat_axis=0, tiled=True)]
    dot_general x4 -> x0, matrix products: 24 us -> none  [the longest x3 17.9 us: shards(): jnp.einsum('rcad,rced->rcae', left_half, margin, preferred_element_type=j...]
    dot_general x15, matrix products: 54.8 us -> 62.7 us  [add_group(): jnp.einsum('rqad,rqbd->rab', ladder_half, factors, preferred_element_type...]
  transfers between devices with their start and end apart: 5 -> 3, of which waited for: 5 -> 3; matrix products, arithmetic and copies ran while one was open for 14% -> 19% of each run, Pallas kernels for 0% -> 0%
where the time goes in v1:
time: 380 us; the launch traced here: 379 us
  waiting for transfers between devices  105 us (28%)
  Pallas kernels  101 us (27%)
  blocking collectives  75.7 us (20%)
  matrix products  62.7 us (16%)
  starting transfers between devices  15.2 us (4%)
  other arithmetic  12.7 us (3%)
  local copies, waits for them, and re-layouts  6.48 us (2%)
    all_to_all x3, waiting for transfers between devices, swap(): lax.all_to_all(values, 'pairs', split_axis=0, concat_axis=0, tiled=True)  105 us
    all_to_all x3, blocking collectives, swap(): lax.all_to_all(values, 'pairs', split_axis=0, concat_axis=0, tiled=True)  75.7 us
    pallas_call x3, Pallas kernels, couple(): pl.pallas_call(functools.partial(couple_kernel, first, last), grid=(steps...  64.9 us
    dot_general x15, matrix products, add_group(): jnp.einsum('rqad,rqbd->rab', ladder_half, factors, preferred_element_type...  62.7 us
    pallas_call x3, Pallas kernels, pick_pieces(): pl.pallas_call(pick_kernel, grid=(groups,), in_specs=[pl.BlockSpec((1, ha...  33.5 us
    all_to_all x3, starting transfers between devices, swap(): lax.all_to_all(values, 'pairs', split_axis=0, concat_axis=0, tiled=True)  15.2 us
  transfers between devices with their start and end apart: 3, of which 3 were waited for; matrix products, arithmetic and copies ran while one was open for 19% of the time, Pallas kernels for 0%

profile of v1, /device:TPU:1, one launch (start us, length us, event | category | flops | bytes accessed | tf_op | source)
XLA Modules:
  0.0 379.4 jit_solution(14179788268715285913)
XLA Ops:
  9.7 35.9 %all_to_all.30 = bf16[128,8,768]{2,1,0:T(8,128)(2,1)S(1)} all-to-all(bf16[128,8,768]{2,1,0:T(8,128)(2,1)} %bitcast.61), channel_id=1, replica_groups=mesh['pairs'=128] {'pairs'}, dimensions={0} | all-to-all | bytes 3145728 | tf_op jit(solution)/shard_map/all_to_all | solution.py:199
  46.8 15.9 %pick_pieces.3 = bf16[128,48,640]{2,1,0:T(8,128)(2,1)} custom-call(s32[8,48,16]{2,1,0:T(8,128)} %bitcast.69, bf16[1024,768]{1,0:T(8,128)(2,1)} %bitcast.63), custom_call_target="tpu_custom_call" | custom-call | flops 8053063680 | bytes 9175040 | tf_op jit(solution)/shard_map/pick_pieces/pallas_call | solution.py:92
  62.7 6.1 %all-to-all-start.1 = ((bf16[128,48,640]{2,1,0:T(8,128)(2,1)}), bf16[128,48,640]{2,1,0:T(8,128)(2,1)}, u32[]{:S(2)}, u32[]{:S(2)}) async-start(bf16[128,48,640]{2,1,0:T(8,128)(2,1)} %pick_pieces.3), calls=%async_computation.1 | async-start | bytes 15728640 | tf_op jit(solution)/shard_map/all_to_all | solution.py:199
  70.5 18.3 %while.42 = (s32[]{:T(128)}, f32[8,128,128]{2,1,0:T(8,128)S(1)}, bf16[8,40,128,128]{3,2,1,0:T(8,128)(2,1)}, bf16[8,128,128]{2,1,0:T(8,128)(2,1)S(1)}, s32[]{:T(128)}, /*index=5*/s32[]{:T(128)}, s32[]{:T(128)}, s32[]{:T(128)}) while((s32[]{:T(128)}, f32[8,128,128]{2,1,0:T(8,128)S(1)}, bf16[8,40,128,128]{3,2,1,0:T(8,128)(2,1)}, ...), condition=%wide.region_1.2_spmd.clone, body=%wide.region_0.1_spmd.clone.sunk | while | flops 538181632 | bytes 5506700 | solution.py:249
  90.2 70.9 %all-to-all-done.1 = bf16[128,48,640]{2,1,0:T(8,128)(2,1)} async-done(((bf16[128,48,640]{2,1,0:T(8,128)(2,1)}), bf16[128,48,640]{2,1,0:T(8,128)(2,1)}, u32[]{:S(2)}, u32[]{:S(2)}) %all-to-all-start.1) | async-done | bytes 7864352 | tf_op jit(solution)/shard_map/all_to_all | solution.py:199
  161.1 29.2 %couple.3 = (f32[8,128,128]{2,1,0:T(8,128)}, bf16[8,128,128]{2,1,0:T(8,128)(2,1)}, bf16[64,2,8,256]{3,2,1,0:T(8,128)(2,1)}, bf16[6,2,8,128,128]{4,3,2,1,0:T(8,128)(2,1)}) custom-call(f32[8,12]{1,0:T(8,128)} %convert_element_type.59.refs_0_, bf16[64,2,6,8,640]{4,3,2,1,0:T(8,128)(2,1)} %bitcast.5.refs_1_, bf16[8,128,192]{2,1,0:T(8,128)(2,1)} %bitcast.62, ...), custom_call_target="tpu_custom_call" | custom-call | tf_op jit(solution)/shard_map/couple/pallas_call | solution.py:177
  190.3 20.8 %all_to_all.31 = bf16[128,8,256]{2,1,0:T(8,128)(2,1)} all-to-all(bf16[128,8,256]{2,1,0:T(8,128)(2,1)} %bitcast.64), channel_id=1, replica_groups=mesh['pairs'=128] {'pairs'}, dimensions={0} | all-to-all | bytes 1048576 | tf_op jit(solution)/shard_map/all_to_all | solution.py:199
  211.2 8.8 %pick_pieces.4 = bf16[128,48,256]{2,1,0:T(8,128)(2,1)} custom-call(s32[8,48,16]{2,1,0:T(8,128)} %bitcast.70, bf16[1024,256]{1,0:T(8,128)(2,1)} %bitcast.67), custom_call_target="tpu_custom_call" | custom-call | flops 3221225472 | bytes 3670016 | tf_op jit(solution)/shard_map/pick_pieces/pallas_call | solution.py:92
  220.0 4.5 %all-to-all-start.3 = ((bf16[128,48,256]{2,1,0:T(8,128)(2,1)}), bf16[128,48,256]{2,1,0:T(8,128)(2,1)S(1)}, u32[]{:S(2)}, u32[]{:S(2)}) async-start(bf16[128,48,256]{2,1,0:T(8,128)(2,1)} %pick_pieces.4), calls=%async_computation.3 | async-start | bytes 6291456 | tf_op jit(solution)/shard_map/all_to_all | solution.py:199
  224.5 22.3 %while.43 = (s32[]{:T(128)}, f32[8,128,128]{2,1,0:T(8,128)}, bf16[8,40,128,128]{3,2,1,0:T(8,128)(2,1)}, bf16[8,128,128]{2,1,0:T(8,128)(2,1)}, s32[]{:T(128)}, /*index=5*/s32[]{:T(128)}, s32[]{:T(128)}, s32[]{:T(128)}) while((s32[]{:T(128)}, f32[8,128,128]{2,1,0:T(8,128)}, bf16[8,40,128,128]{3,2,1,0:T(8,128)(2,1)}, ...), condition=%wide.region_3.4_spmd.clone, body=%wide.region_2.3_spmd.clone.sunk | while | flops 538181632 | bytes 5506700 | solution.py:249
  228.9 4.5 %fusion.100 = f32[8,128,128]{2,1,0:T(8,128)} fusion(bf16[8,40,128,128]{3,2,1,0:T(8,128)(2,1)} %get-tuple-element.451, s32[]{:T(128)S(6)} %select_n.28, f32[8,128,128]{2,1,0:T(8,128)} %get-tuple-element.442, bf16[8,128,128]{2,1,0:T(8,128)(2,1)} %get-tuple-element.452, pred[]{:T(512)S(6)} %compare.11), kind=kOutput, calls=%fused_computation.13.clone.1 | convolution fusion | flops 538181632 | bytes 5506560 | tf_op jit(solution)/shard_map/while/body/eval_jaxpr/rqad,rqbd->rab/dot_general | solution.py:245
  233.5 4.5 %fusion.100 = f32[8,128,128]{2,1,0:T(8,128)} fusion(bf16[8,40,128,128]{3,2,1,0:T(8,128)(2,1)} %get-tuple-element.451, s32[]{:T(128)S(6)} %select_n.28, f32[8,128,128]{2,1,0:T(8,128)} %get-tuple-element.442, bf16[8,128,128]{2,1,0:T(8,128)(2,1)} %get-tuple-element.452, pred[]{:T(512)S(6)} %compare.11), kind=kOutput, calls=%fused_computation.13.clone.1 | convolution fusion | flops 538181632 | bytes 5506560 | tf_op jit(solution)/shard_map/while/body/eval_jaxpr/rqad,rqbd->rab/dot_general | solution.py:245
  237.9 4.4 %fusion.100 = f32[8,128,128]{2,1,0:T(8,128)} fusion(bf16[8,40,128,128]{3,2,1,0:T(8,128)(2,1)} %get-tuple-element.451, s32[]{:T(128)S(6)} %select_n.28, f32[8,128,128]{2,1,0:T(8,128)} %get-tuple-element.442, bf16[8,128,128]{2,1,0:T(8,128)(2,1)} %get-tuple-element.452, pred[]{:T(512)S(6)} %compare.11), kind=kOutput, calls=%fused_computation.13.clone.1 | convolution fusion | flops 538181632 | bytes 5506560 | tf_op jit(solution)/shard_map/while/body/eval_jaxpr/rqad,rqbd->rab/dot_general | solution.py:245
  249.1 17.1 %all-to-all-done.3 = bf16[128,48,256]{2,1,0:T(8,128)(2,1)S(1)} async-done(((bf16[128,48,256]{2,1,0:T(8,128)(2,1)}), bf16[128,48,256]{2,1,0:T(8,128)(2,1)S(1)}, u32[]{:S(2)}, u32[]{:S(2)}) %all-to-all-start.3) | async-done | bytes 3145760 | tf_op jit(solution)/shard_map/all_to_all | solution.py:199
  267.9 18.2 %couple.4 = (f32[8,128,128]{2,1,0:T(8,128)}, bf16[8,128,128]{2,1,0:T(8,128)(2,1)}, bf16[64,2,8,256]{3,2,1,0:T(8,128)(2,1)}) custom-call(f32[8,12]{1,0:T(8,128)} %convert_element_type.59.refs_0_, bf16[64,2,6,8,256]{4,3,2,1,0:T(8,128)(2,1)} %bitcast.59, bf16[6,2,8,128,128]{4,3,2,1,0:T(8,128)(2,1)} %get-tuple-element.251.refs_2_, ...), custom_call_target="tpu_custom_call" | custom-call | tf_op jit(solution)/shard_map/couple/pallas_call | solution.py:177
  286.1 19.0 %all_to_all.32 = bf16[128,8,256]{2,1,0:T(8,128)(2,1)} all-to-all(bf16[128,8,256]{2,1,0:T(8,128)(2,1)} %bitcast.65), channel_id=1, replica_groups=mesh['pairs'=128] {'pairs'}, dimensions={0} | all-to-all | bytes 1048576 | tf_op jit(solution)/shard_map/all_to_all | solution.py:199
  305.1 8.8 %pick_pieces.5 = bf16[128,48,256]{2,1,0:T(8,128)(2,1)} custom-call(s32[8,48,16]{2,1,0:T(8,128)} %bitcast.71, bf16[1024,256]{1,0:T(8,128)(2,1)} %bitcast.66), custom_call_target="tpu_custom_call" | custom-call | flops 3221225472 | bytes 3670016 | tf_op jit(solution)/shard_map/pick_pieces/pallas_call | solution.py:92
  313.9 4.5 %all-to-all-start.5 = ((bf16[128,48,256]{2,1,0:T(8,128)(2,1)}), bf16[128,48,256]{2,1,0:T(8,128)(2,1)S(1)}, u32[]{:S(2)}, u32[]{:S(2)}) async-start(bf16[128,48,256]{2,1,0:T(8,128)(2,1)} %pick_pieces.5), calls=%async_computation.5 | async-start | bytes 6291456 | tf_op jit(solution)/shard_map/all_to_all | solution.py:199
  318.5 22.3 %while.44 = (s32[]{:T(128)}, f32[8,128,128]{2,1,0:T(8,128)}, bf16[8,40,128,128]{3,2,1,0:T(8,128)(2,1)}, bf16[8,128,128]{2,1,0:T(8,128)(2,1)}, s32[]{:T(128)}, /*index=5*/s32[]{:T(128)}, s32[]{:T(128)}, s32[]{:T(128)}) while((s32[]{:T(128)}, f32[8,128,128]{2,1,0:T(8,128)}, bf16[8,40,128,128]{3,2,1,0:T(8,128)(2,1)}, ...), condition=%wide.region_5.6_spmd.clone, body=%wide.region_4.5_spmd.clone.sunk | while | flops 538181632 | bytes 5506700 | solution.py:249
  322.9 4.5 %fusion.105 = f32[8,128,128]{2,1,0:T(8,128)} fusion(bf16[8,40,128,128]{3,2,1,0:T(8,128)(2,1)} %get-tuple-element.475, s32[]{:T(128)S(6)} %select_n.29, f32[8,128,128]{2,1,0:T(8,128)} %get-tuple-element.466, bf16[8,128,128]{2,1,0:T(8,128)(2,1)} %get-tuple-element.476, pred[]{:T(512)S(6)} %compare.12), kind=kOutput, calls=%fused_computation.21.clone.1 | convolution fusion | flops 538181632 | bytes 5506560 | tf_op jit(solution)/shard_map/while/body/eval_jaxpr/rqad,rqbd->rab/dot_general | solution.py:245
  327.4 4.5 %fusion.105 = f32[8,128,128]{2,1,0:T(8,128)} fusion(bf16[8,40,128,128]{3,2,1,0:T(8,128)(2,1)} %get-tuple-element.475, s32[]{:T(128)S(6)} %select_n.29, f32[8,128,128]{2,1,0:T(8,128)} %get-tuple-element.466, bf16[8,128,128]{2,1,0:T(8,128)(2,1)} %get-tuple-element.476, pred[]{:T(512)S(6)} %compare.12), kind=kOutput, calls=%fused_computation.21.clone.1 | convolution fusion | flops 538181632 | bytes 5506560 | tf_op jit(solution)/shard_map/while/body/eval_jaxpr/rqad,rqbd->rab/dot_general | solution.py:245
  331.9 4.4 %fusion.105 = f32[8,128,128]{2,1,0:T(8,128)} fusion(bf16[8,40,128,128]{3,2,1,0:T(8,128)(2,1)} %get-tuple-element.475, s32[]{:T(128)S(6)} %select_n.29, f32[8,128,128]{2,1,0:T(8,128)} %get-tuple-element.466, bf16[8,128,128]{2,1,0:T(8,128)(2,1)} %get-tuple-element.476, pred[]{:T(512)S(6)} %compare.12), kind=kOutput, calls=%fused_computation.21.clone.1 | convolution fusion | flops 538181632 | bytes 5506560 | tf_op jit(solution)/shard_map/while/body/eval_jaxpr/rqad,rqbd->rab/dot_general | solution.py:245
  343.1 17.1 %all-to-all-done.5 = bf16[128,48,256]{2,1,0:T(8,128)(2,1)S(1)} async-done(((bf16[128,48,256]{2,1,0:T(8,128)(2,1)}), bf16[128,48,256]{2,1,0:T(8,128)(2,1)S(1)}, u32[]{:S(2)}, u32[]{:S(2)}) %all-to-all-start.5) | async-done | bytes 3145760 | tf_op jit(solution)/shard_map/all_to_all | solution.py:199
  361.9 17.5 %couple.5 = f32[8,128,128]{2,1,0:T(8,128)} custom-call(f32[8,12]{1,0:T(8,128)} %convert_element_type.59.refs_0_, bf16[64,2,6,8,256]{4,3,2,1,0:T(8,128)(2,1)} %bitcast.60, bf16[6,2,8,128,128]{4,3,2,1,0:T(8,128)(2,1)} %get-tuple-element.251.refs_2_, f32[8,128,128]{2,1,0:T(8,128)} %get-tuple-element.256.refs_3_, f32[8,128,128]{2,1,0:T(8,128)} %add_add_fusion.refs_4_, ...), custom_call_target="tpu_custom_call" | custom-call | tf_op jit(solution)/shard_map/couple/pallas_call | solution.py:177
  (49 shorter events, 57.8 us)
Async XLA Ops:
  45.6 1.3 copy-start.4
  62.7 6.1 %copy-start.3 = (bf16[8,192,128]{2,1,0:T(8,128)(2,1)S(1)}, bf16[8,192,128]{2,1,0:T(8,128)(2,1)}, u32[]{:S(2)}) copy-start(bf16[8,192,128]{2,1,0:T(8,128)(2,1)} %broadcast_multiply_fusion.basis_ref) | copy-start | bytes 1179652
  62.7 7.2 %copy-start.7 = (bf16[8,12]{1,0:T(8,128)(2,1)S(1)}, bf16[8,12]{1,0:T(8,128)(2,1)}, u32[]{:S(2)}) copy-start(bf16[8,12]{1,0:T(8,128)(2,1)} %param.23) | copy-start | bytes 580
  62.7 98.4 %all-to-all-start.1 = ((bf16[128,48,640]{2,1,0:T(8,128)(2,1)}), bf16[128,48,640]{2,1,0:T(8,128)(2,1)}, u32[]{:S(2)}, u32[]{:S(2)}) async-start(bf16[128,48,640]{2,1,0:T(8,128)(2,1)} %pick_pieces.3), calls=%async_computation.1 | async-start | bytes 15728640 | tf_op jit(solution)/shard_map/all_to_all | solution.py:199
  70.5 18.4 %copy-start.2 = (bf16[8,128,128]{2,1,0:T(8,128)(2,1)S(1)}, bf16[8,128,128]{2,1,0:T(8,128)(2,1)}, u32[]{:S(2)}) copy-start(bf16[8,128,128]{2,1,0:T(8,128)(2,1)} %param.19) | copy-start | bytes 786436
  70.5 18.4 %copy-start.5 = (f32[8,128]{1,0:T(8,128)S(1)}, f32[8,128]{1,0:T(8,128)}, u32[]{:S(2)}) copy-start(f32[8,128]{1,0:T(8,128)} %param.21) | copy-start | bytes 12292
  70.5 18.4 %copy-start.6 = (f32[8]{0:T(128)S(1)}, f32[8]{0:T(128)}, u32[]{:S(2)}) copy-start(f32[8]{0:T(128)} %param.22) | copy-start | bytes 100
  220.0 46.3 %all-to-all-start.3 = ((bf16[128,48,256]{2,1,0:T(8,128)(2,1)}), bf16[128,48,256]{2,1,0:T(8,128)(2,1)S(1)}, u32[]{:S(2)}, u32[]{:S(2)}) async-start(bf16[128,48,256]{2,1,0:T(8,128)(2,1)} %pick_pieces.4), calls=%async_computation.3 | async-start | bytes 6291456 | tf_op jit(solution)/shard_map/all_to_all | solution.py:199
  266.2 1.6 copy-start
  313.9 46.3 %all-to-all-start.5 = ((bf16[128,48,256]{2,1,0:T(8,128)(2,1)}), bf16[128,48,256]{2,1,0:T(8,128)(2,1)S(1)}, u32[]{:S(2)}, u32[]{:S(2)}) async-start(bf16[128,48,256]{2,1,0:T(8,128)(2,1)} %pick_pieces.5), calls=%async_computation.5 | async-start | bytes 6291456 | tf_op jit(solution)/shard_map/all_to_all | solution.py:199
  360.2 1.6 copy-start.1

commit v2 on v1

v2 whole, which is shorter than its diff:
```python
import functools

import jax
import jax.numpy as jnp
from jax import lax
from jax.experimental import pallas as pl
from jax.experimental.pallas import tpu as pltpu
from jax.sharding import PartitionSpec as P

ITERS = 3
LEVEL_SHIFT = 0.3
LANES = 128
TURN = 32
F32 = jnp.float32
BF16 = jnp.bfloat16
NT = (((1,), (1,)), ((), ()))


def regroup(major, minor, turned):
    size = major * minor
    row = lax.broadcasted_iota(jnp.int32, (size, size), 0)
    col = lax.broadcasted_iota(jnp.int32, (size, size), 1)
    to, source = (col, row) if turned else (row, col)
    hit = source == lax.rem(to, major) * minor + lax.div(to, major)
    return jnp.where(hit, 1.0, 0.0).astype(BF16)


def part(values, index):
    return values[:, index * LANES : (index + 1) * LANES]


def store_pieces(stack, send_ref, first_lane):
    chips, _, own, _ = send_ref.shape
    parts = stack[0].shape[0] // chips
    back = regroup(TURN, own, True)
    for start in range(0, chips, TURN):
        rows = jnp.concatenate(
            [
                jnp.concatenate(
                    [m[i * chips + start : i * chips + start + TURN] for i in range(parts)], axis=1
                )
                for m in stack
            ],
            axis=0,
        )
        pieces = jnp.dot(back, rows, preferred_element_type=F32).astype(BF16)
        pieces = pieces.reshape(TURN, own, parts * LANES)
        for core in range(2):
            send_ref[start : start + TURN, core, :, first_lane : first_lane + parts * LANES] = (
                pieces
            )


def start_kernel(
    count_ref, occ_ref, owner_ref, local_ref, basis_ref, exchange_ref, energy_ref,
    amp_ref, sent_ref, turned_ref, send_ref,
):
    chips, _, own, width = send_ref.shape
    domain, orbitals = basis_ref.shape[1:]
    row = lax.broadcasted_iota(jnp.int32, (orbitals, orbitals), 0)
    col = lax.broadcasted_iota(jnp.int32, (orbitals, orbitals), 1)
    basis_col = lax.broadcasted_iota(jnp.int32, (domain, orbitals), 1)
    stack = []
    for p in range(own):
        count = count_ref[p]
        live = jnp.logical_and(row < count, col < count)
        energy = jnp.broadcast_to(energy_ref[p : p + 1, :], (orbitals, orbitals))
        energy_sum = energy.T + energy - occ_ref[p]
        driving = jnp.where(live, exchange_ref[p].astype(F32), 0.0)
        amplitudes = -driving / (energy_sum + LEVEL_SHIFT)
        amp_ref[p] = amplitudes
        sent = amplitudes.astype(BF16)
        sent_ref[p] = sent
        masked = jnp.where(basis_col < count, basis_ref[p].astype(F32), 0.0)
        turned_ref[p] = masked.T.astype(BF16)
        stack.append(jnp.concatenate([sent, masked.astype(BF16)], axis=0))
    store_pieces(stack, send_ref, 0)
    half = owner_ref.shape[1] // 2
    empty = jnp.zeros((own, LANES - 2 * half), F32)
    for core in range(2):
        mine = slice(core * half, (core + 1) * half)
        asked = jnp.concatenate(
            [owner_ref[:, mine].astype(F32), local_ref[:, mine].astype(F32), empty], axis=1
        )
        send_ref[:, core, :, width - LANES :] = jnp.broadcast_to(
            asked.astype(BF16)[None], (chips, own, LANES)
        )


def start(count, occ, owner, local, basis, exchange, energy, chips):
    own, domain, orbitals = basis.shape
    width = ((orbitals + domain) // chips + 1) * LANES
    scalars, vectors = pl.BlockSpec(memory_space=pltpu.SMEM), pl.BlockSpec(memory_space=pltpu.VMEM)
    return pl.pallas_call(
        start_kernel,
        in_specs=[scalars] * 2 + [vectors] * 5,
        out_specs=[vectors] * 4,
        out_shape=[
            jax.ShapeDtypeStruct((own, orbitals, orbitals), F32),
            jax.ShapeDtypeStruct((own, orbitals, orbitals), BF16),
            jax.ShapeDtypeStruct((own, orbitals, domain), BF16),
            jax.ShapeDtypeStruct((chips, 2, own, width), BF16),
        ],
        name="start",
    )(count, occ, owner, local, basis, exchange, energy)


def pick_kernel(list_ref, table_ref, out_ref, onehot_ref):
    half, group = list_ref.shape[1:]
    rows, width = table_ref.shape
    lane = lax.broadcasted_iota(jnp.int32, (half, LANES), 1).astype(F32).astype(BF16)
    one, zero = jnp.bfloat16(1), jnp.bfloat16(0)
    at_once = 4
    for begin in range(0, group, at_once):
        for member in range(begin, begin + at_once):
            wanted = jnp.broadcast_to(list_ref[0, :, member : member + 1], (half, LANES))
            tile_of = lax.shift_right_logical(wanted, 7).astype(F32).astype(BF16)
            lane_of = jnp.bitwise_and(wanted, LANES - 1).astype(F32).astype(BF16)
            hit = jnp.where(lane_of == lane, one, zero)
            for tile in range(rows // LANES):
                onehot_ref[
                    member * half : (member + 1) * half, tile * LANES : (tile + 1) * LANES
                ] = jnp.where(tile_of == jnp.bfloat16(tile), hit, zero)
        picked = jnp.dot(
            onehot_ref[begin * half : (begin + at_once) * half],
            table_ref[...],
            preferred_element_type=F32,
        )
        out_ref[begin : begin + at_once] = picked.astype(BF16).reshape(at_once, half, width)


def pick_pieces(lists, table, width):
    groups, half, group = lists.shape
    rows = table.shape[0]
    return pl.pallas_call(
        pick_kernel,
        grid=(groups,),
        in_specs=[
            pl.BlockSpec((1, half, group), lambda g: (g, 0, 0)),
            pl.BlockSpec((rows, width), lambda g: (0, 0)),
        ],
        out_specs=pl.BlockSpec((group, half, width), lambda g: (g, 0, 0)),
        out_shape=jax.ShapeDtypeStruct((groups * group, half, width), BF16),
        scratch_shapes=[pltpu.VMEM((group * half, rows), BF16)],
        cost_estimate=pl.CostEstimate(
            flops=2 * groups * group * half * rows * width,
            bytes_accessed=2 * (rows * width + groups * group * half * width),
            transcendentals=0,
        ),
        name="pick_pieces",
    )(lists, table)


def couple_kernel(first, last, *refs):
    refs = list(refs)
    weight_ref, arrived_hbm, margin_hbm = refs[:3]
    amp_hbm, rest_hbm, div_hbm, out_ref = refs[3:7]
    refs = refs[7:]
    if not last:
        sent_ref, send_ref = refs[:2]
        refs = refs[2:]
    if first:
        margin_ref, refs = refs[0], refs[1:]
    other_ref, left_ref, held_ref, amp_ref, rest_ref, div_ref, sems = refs[:7]
    if first:
        turned_ref, basis_ref, arrived_ref = held_ref, refs[7], refs[8]
    else:
        margin_ref, arrived_ref = held_ref, arrived_hbm
    chips, _, steps, own, width = arrived_ref.shape
    orbitals = amp_ref.shape[1]
    blocks = chips // TURN
    copies = []
    if first:
        for i in range(blocks):
            rows = pl.ds(i * TURN, TURN)
            copies.append(
                pltpu.make_async_copy(arrived_hbm.at[rows], arrived_ref.at[rows], sems.at[i])
            )
    for i, (source, target) in enumerate(
        [(margin_hbm, held_ref), (amp_hbm, amp_ref), (rest_hbm, rest_ref), (div_hbm, div_ref)]
    ):
        copies.append(pltpu.make_async_copy(source, target, sems.at[blocks + i]))
    landed = copies[:-4]
    copies = copies[-4:]
    for copy in landed + copies:
        copy.start()
    order = regroup(TURN, own, False)
    for block in range(blocks):
        begin = block * TURN
        if first:
            landed[block].wait()
        for step in range(steps):
            for core in range(2):
                c = core * steps + step
                arrived = arrived_ref[begin : begin + TURN, core, step].reshape(TURN * own, width)
                moved = jnp.dot(order, arrived, preferred_element_type=F32).astype(BF16)
                for p in range(own):
                    rows = moved[p * TURN : (p + 1) * TURN]
                    for i in range(orbitals // chips):
                        place = i * chips + begin
                        other_ref[p, c, place : place + TURN, :] = part(rows, i)
                    for i in range(orbitals // chips, width // LANES):
                        place = i * chips + begin - orbitals
                        basis_ref[p, place : place + TURN, c * LANES : (c + 1) * LANES] = part(
                            rows, i
                        )
    copies[0].wait()
    for p in range(own):
        if first:
            margin_ref[p] = jnp.dot(
                turned_ref[p], basis_ref[p], preferred_element_type=F32
            ).astype(BF16)
        for c in range(2 * steps):
            left = jnp.dot(
                margin_ref[p, :, c * orbitals : (c + 1) * orbitals],
                other_ref[p, c],
                preferred_element_type=F32,
            )
            left_ref[p, :, c * orbitals : (c + 1) * orbitals] = (left * weight_ref[p, c]).astype(
                BF16
            )
    for copy in copies[1:]:
        copy.wait()
    stack = []
    for p in range(own):
        coupled = lax.dot_general(left_ref[p], margin_ref[p], NT, preferred_element_type=F32)
        amplitudes = amp_ref[p] - (rest_ref[p] + coupled) / div_ref[p]
        out_ref[p] = amplitudes
        if not last:
            sent = amplitudes.astype(BF16)
            sent_ref[p] = sent
            stack.append(sent)
    if not last:
        store_pieces(stack, send_ref, 0)


def couple(first, last, weights, arrived, margin, amplitudes, rest, divisor):
    chips, _, steps, own, width = arrived.shape
    orbitals = amplitudes.shape[1]
    vectors = pl.BlockSpec(memory_space=pltpu.VMEM)
    far = pl.BlockSpec(memory_space=pltpu.HBM)
    all_columns = 2 * steps * orbitals
    out_shape = [jax.ShapeDtypeStruct(amplitudes.shape, F32)]
    scratch_shapes = [
        pltpu.VMEM((own, 2 * steps, orbitals, orbitals), BF16),
        pltpu.VMEM((own, orbitals, all_columns), BF16),
        pltpu.VMEM(margin.shape, BF16),
        pltpu.VMEM(amplitudes.shape, F32),
        pltpu.VMEM(amplitudes.shape, F32),
        pltpu.VMEM(amplitudes.shape, F32),
        pltpu.SemaphoreType.DMA((chips // TURN + 4,)),
    ]
    if not last:
        out_shape += [
            jax.ShapeDtypeStruct(amplitudes.shape, BF16),
            jax.ShapeDtypeStruct((chips, 2, own, orbitals // chips * LANES), BF16),
        ]
    if first:
        out_shape.append(jax.ShapeDtypeStruct((own, orbitals, all_columns), BF16))
        scratch_shapes.append(pltpu.VMEM((own, margin.shape[2], all_columns), BF16))
        scratch_shapes.append(pltpu.VMEM(arrived.shape, BF16))
    return pl.pallas_call(
        functools.partial(couple_kernel, first, last),
        in_specs=[pl.BlockSpec(memory_space=pltpu.SMEM), far if first else vectors] + [far] * 4,
        out_specs=[vectors] * len(out_shape),
        out_shape=out_shape,
        scratch_shapes=scratch_shapes,
        compiler_params=None if first else pltpu.CompilerParams(vmem_limit_bytes=48 << 20),
        name="couple",
    )(weights, arrived, margin, amplitudes, rest, divisor)


def swap(values):
    return lax.all_to_all(values, "pairs", split_axis=0, concat_axis=0, tiled=True)


def shards(
    pno_basis,
    pno_count,
    partner_owner,
    partner_local,
    exchange_k,
    ladder_factor,
    pno_energy,
    occ_energy,
    coupling_fock,
):
    devices = lax.axis_size("pairs")
    chips = devices // 2
    own, domain, orbitals = pno_basis.shape
    fitted = ladder_factor.shape[1]
    partners = partner_owner.shape[1]
    half = own * partners // 2
    rows = devices * own
    group = 32
    columns = lax.broadcasted_iota(jnp.int32, (own, orbitals), 1)
    live_cols = (columns < pno_count[:, None]).astype(F32)
    energy_sum = pno_energy[:, :, None] + pno_energy[:, None, :] - occ_energy[:, None, None]
    divisor = energy_sum + LEVEL_SHIFT
    driving = exchange_k.astype(F32) * (live_cols[:, :, None] * live_cols[:, None, :])
    weights = coupling_fock.astype(F32)

    def ladder_of(sent):
        group_width = 8

        def add_group(group_index, total):
            factors = lax.dynamic_slice_in_dim(
                ladder_factor, group_index * group_width, group_width, 1
            )
            ladder_half = jnp.einsum(
                "rqac,rcd->rqad", factors, sent, preferred_element_type=F32
            ).astype(BF16)
            return total + jnp.einsum(
                "rqad,rqbd->rab", ladder_half, factors, preferred_element_type=F32
            )

        return lax.fori_loop(
            0, fitted // group_width, add_group, jnp.zeros((own, orbitals, orbitals), F32)
        )

    amplitudes, sent, margin, send = start(
        pno_count, occ_energy, partner_owner, partner_local, pno_basis, exchange_k, pno_energy, chips
    )
    lists = None
    for iteration in range(ITERS):
        first, last = iteration == 0, iteration == ITERS - 1
        held = swap(send.reshape(devices, own, send.shape[-1]))
        width = 2 * LANES
        if first:
            width = held.shape[-1] - LANES
            names = held[:, :, width : width + partners].astype(jnp.int32)
            lists = names[:, :, : partners // 2] * own + names[:, :, partners // 2 :]
            lists = lists.reshape(devices // group, group, own, partners // 2)
            lists = jnp.transpose(lists, (0, 3, 2, 1)).reshape(devices // group, half, group)
        arrived = swap(pick_pieces(lists, held.reshape(rows, held.shape[-1]), width))
        rest = driving + energy_sum * amplitudes + ladder_of(sent)
        results = couple(
            first,
            last,
            weights,
            arrived.reshape(chips, 2, partners // 2, own, width),
            margin,
            amplitudes,
            rest,
            divisor,
        )
        amplitudes = results[0]
        if not last:
            sent, send = results[1], results[2]
        if first:
            margin = results[3]
    return amplitudes


def solution(mesh):
    return jax.shard_map(
        shards,
        mesh=mesh,
        in_specs=(
            P("pairs", None, None),
            P("pairs"),
            P("pairs", None),
            P("pairs", None),
            P("pairs", None, None),
            P("pairs", None, None, None),
            P("pairs", None),
            P("pairs"),
            P("pairs", None),
        ),
        out_specs=P("pairs", None, None),
        check_vma=False,
    )
```

time: 380 us -> 328 us (0.86)
  Pallas kernels: 101 us -> 52.1 us
  other arithmetic: 12.7 us -> 6.68 us
    pallas_call x4, Pallas kernels: 67.7 us -> 23.8 us  [the longest x3 20.8 us: couple(): pl.pallas_call(functools.partial(couple_kernel, first, last), in_specs=[p...]
    pallas_call x3, Pallas kernels: 33.5 us -> 28.4 us  [pick_pieces(): pl.pallas_call(pick_kernel, grid=(groups,), in_specs=[pl.BlockSpec((1, ha...]
    unnamed x16 -> x31, local copies, waits for them, and re-layouts: 3.45 us -> 7.27 us
  transfers between devices with their start and end apart: 3 -> 3, of which waited for: 3 -> 3; matrix products, arithmetic and copies ran while one was open for 19% -> 21% of each run, Pallas kernels for 0% -> 0%
where the time goes in v2:
time: 328 us; the launch traced here: 326 us
  waiting for transfers between devices  106 us (32%)
  blocking collectives  74.9 us (23%)
  matrix products  62.7 us (19%)
  Pallas kernels  52.1 us (16%)
  starting transfers between devices  15.2 us (5%)
  local copies, waits for them, and re-layouts  8.22 us (3%)
  other arithmetic  6.68 us (2%)
    all_to_all x3, waiting for transfers between devices, swap(): lax.all_to_all(values, 'pairs', split_axis=0, concat_axis=0, tiled=True)  106 us
    all_to_all x3, blocking collectives, swap(): lax.all_to_all(values, 'pairs', split_axis=0, concat_axis=0, tiled=True)  74.9 us
    dot_general x15, matrix products, add_group(): jnp.einsum('rqad,rqbd->rab', ladder_half, factors, preferred_element_type...  62.7 us
    pallas_call x3, Pallas kernels, pick_pieces(): pl.pallas_call(pick_kernel, grid=(groups,), in_specs=[pl.BlockSpec((1, ha...  28.4 us
    pallas_call x3, Pallas kernels, couple(): pl.pallas_call(functools.partial(couple_kernel, first, last), in_specs=[p...  20.8 us
    all_to_all x3, starting transfers between devices, swap(): lax.all_to_all(values, 'pairs', split_axis=0, concat_axis=0, tiled=True)  15.2 us
    unnamed x31, local copies, waits for them, and re-layouts  7.27 us
  transfers between devices with their start and end apart: 3, of which 3 were waited for; matrix products, arithmetic and copies ran while one was open for 21% of the time, Pallas kernels for 0%

profile of v2, /device:TPU:1, one launch (start us, length us, event | category | flops | bytes accessed | tf_op | source)
XLA Modules:
  0.0 326.4 jit_solution(1987787060880695449)
XLA Ops:
  3.0 35.9 %all_to_all.30 = bf16[128,8,768]{2,1,0:T(8,128)(2,1)S(1)} all-to-all(bf16[128,8,768]{2,1,0:T(8,128)(2,1)} %bitcast.64), channel_id=1, replica_groups=mesh['pairs'=128] {'pairs'}, dimensions={0} | all-to-all | bytes 3145728 | tf_op jit(solution)/shard_map/all_to_all | solution.py:274
  40.1 13.9 %pick_pieces.3 = bf16[128,48,640]{2,1,0:T(8,128)(2,1)} custom-call(s32[4,48,32]{2,1,0:T(8,128)} %bitcast.69, bf16[1024,768]{1,0:T(8,128)(2,1)} %bitcast.63), custom_call_target="tpu_custom_call" | custom-call | flops 8053063680 | bytes 9175040 | tf_op jit(solution)/shard_map/pick_pieces/pallas_call | solution.py:135
  53.9 6.1 %all-to-all-start.1 = ((bf16[128,48,640]{2,1,0:T(8,128)(2,1)}), bf16[128,48,640]{2,1,0:T(8,128)(2,1)}, u32[]{:S(2)}, u32[]{:S(2)}) async-start(bf16[128,48,640]{2,1,0:T(8,128)(2,1)} %pick_pieces.3), calls=%async_computation.1 | async-start | bytes 15728640 | tf_op jit(solution)/shard_map/all_to_all | solution.py:274
  60.8 18.5 %while.42 = (s32[]{:T(128)}, f32[8,128,128]{2,1,0:T(8,128)S(1)}, bf16[8,40,128,128]{3,2,1,0:T(8,128)(2,1)}, bf16[8,128,128]{2,1,0:T(8,128)(2,1)S(1)}, s32[]{:T(128)}, /*index=5*/s32[]{:T(128)}, s32[]{:T(128)}, s32[]{:T(128)}) while((s32[]{:T(128)}, f32[8,128,128]{2,1,0:T(8,128)S(1)}, bf16[8,40,128,128]{3,2,1,0:T(8,128)(2,1)}, ...), condition=%wide.region_1.0_spmd.clone, body=%wide.region_0.0_spmd.clone.sunk | while | flops 538181632 | bytes 5506708 | solution.py:317
  80.6 71.7 %all-to-all-done.1 = bf16[128,48,640]{2,1,0:T(8,128)(2,1)} async-done(((bf16[128,48,640]{2,1,0:T(8,128)(2,1)}), bf16[128,48,640]{2,1,0:T(8,128)(2,1)}, u32[]{:S(2)}, u32[]{:S(2)}) %all-to-all-start.1) | async-done | bytes 7864352 | tf_op jit(solution)/shard_map/all_to_all | solution.py:274
  152.3 10.3 %couple.3 = (f32[8,128,128]{2,1,0:T(8,128)}, bf16[8,128,128]{2,1,0:T(8,128)(2,1)}, bf16[64,2,8,256]{3,2,1,0:T(8,128)(2,1)}, bf16[8,128,1536]{2,1,0:T(8,128)(2,1)}) custom-call(f32[8,12]{1,0:T(8,128)} %convert_element_type.41.refs_0_, bf16[64,2,6,8,640]{4,3,2,1,0:T(8,128)(2,1)} %bitcast.4.refs_1_, bf16[8,128,192]{2,1,0:T(8,128)(2,1)} %get-tuple-element.254.refs_2_, ...), custom_call_target="tpu_custom_call" | custom-call | tf_op jit(solution)/shard_map/couple/pallas_call | solution.py:262
  162.6 20.9 %all_to_all.31 = bf16[128,8,256]{2,1,0:T(8,128)(2,1)} all-to-all(bf16[128,8,256]{2,1,0:T(8,128)(2,1)} %bitcast.65), channel_id=1, replica_groups=mesh['pairs'=128] {'pairs'}, dimensions={0} | all-to-all | bytes 1048576 | tf_op jit(solution)/shard_map/all_to_all | solution.py:274
  183.4 7.3 %pick_pieces.4 = bf16[128,48,256]{2,1,0:T(8,128)(2,1)} custom-call(s32[4,48,32]{2,1,0:T(8,128)} %bitcast.70, bf16[1024,256]{1,0:T(8,128)(2,1)} %bitcast.67), custom_call_target="tpu_custom_call" | custom-call | flops 3221225472 | bytes 3670016 | tf_op jit(solution)/shard_map/pick_pieces/pallas_call | solution.py:135
  190.7 4.5 %all-to-all-start.3 = ((bf16[128,48,256]{2,1,0:T(8,128)(2,1)}), bf16[128,48,256]{2,1,0:T(8,128)(2,1)S(1)}, u32[]{:S(2)}, u32[]{:S(2)}) async-start(bf16[128,48,256]{2,1,0:T(8,128)(2,1)} %pick_pieces.4), calls=%async_computation.3 | async-start | bytes 6291456 | tf_op jit(solution)/shard_map/all_to_all | solution.py:274
  195.2 22.2 %while.43 = (s32[]{:T(128)}, f32[8,128,128]{2,1,0:T(8,128)}, bf16[8,40,128,128]{3,2,1,0:T(8,128)(2,1)}, bf16[8,128,128]{2,1,0:T(8,128)(2,1)}, s32[]{:T(128)}, /*index=5*/s32[]{:T(128)}, s32[]{:T(128)}, s32[]{:T(128)}) while((s32[]{:T(128)}, f32[8,128,128]{2,1,0:T(8,128)}, bf16[8,40,128,128]{3,2,1,0:T(8,128)(2,1)}, ...), condition=%wide.region_3.0_spmd.clone, body=%wide.region_2.0_spmd.clone.sunk | while | flops 538181632 | bytes 5506708 | solution.py:317
  199.6 4.5 %fusion.98 = f32[8,128,128]{2,1,0:T(8,128)} fusion(bf16[8,40,128,128]{3,2,1,0:T(8,128)(2,1)} %get-tuple-element.455, s32[]{:T(128)S(6)} %select_n.28, f32[8,128,128]{2,1,0:T(8,128)} %get-tuple-element.446, bf16[8,128,128]{2,1,0:T(8,128)(2,1)} %get-tuple-element.456, pred[]{:T(512)S(6)} %compare.10), kind=kOutput, calls=%fused_computation.13.clone.1 | convolution fusion | flops 538181632 | bytes 5506560 | tf_op jit(solution)/shard_map/while/body/eval_jaxpr/rqad,rqbd->rab/dot_general | solution.py:313
  204.1 4.5 %fusion.98 = f32[8,128,128]{2,1,0:T(8,128)} fusion(bf16[8,40,128,128]{3,2,1,0:T(8,128)(2,1)} %get-tuple-element.455, s32[]{:T(128)S(6)} %select_n.28, f32[8,128,128]{2,1,0:T(8,128)} %get-tuple-element.446, bf16[8,128,128]{2,1,0:T(8,128)(2,1)} %get-tuple-element.456, pred[]{:T(512)S(6)} %compare.10), kind=kOutput, calls=%fused_computation.13.clone.1 | convolution fusion | flops 538181632 | bytes 5506560 | tf_op jit(solution)/shard_map/while/body/eval_jaxpr/rqad,rqbd->rab/dot_general | solution.py:313
  208.6 4.5 %fusion.98 = f32[8,128,128]{2,1,0:T(8,128)} fusion(bf16[8,40,128,128]{3,2,1,0:T(8,128)(2,1)} %get-tuple-element.455, s32[]{:T(128)S(6)} %select_n.28, f32[8,128,128]{2,1,0:T(8,128)} %get-tuple-element.446, bf16[8,128,128]{2,1,0:T(8,128)(2,1)} %get-tuple-element.456, pred[]{:T(512)S(6)} %compare.10), kind=kOutput, calls=%fused_computation.13.clone.1 | convolution fusion | flops 538181632 | bytes 5506560 | tf_op jit(solution)/shard_map/while/body/eval_jaxpr/rqad,rqbd->rab/dot_general | solution.py:313
  219.8 17.2 %all-to-all-done.3 = bf16[128,48,256]{2,1,0:T(8,128)(2,1)S(1)} async-done(((bf16[128,48,256]{2,1,0:T(8,128)(2,1)}), bf16[128,48,256]{2,1,0:T(8,128)(2,1)S(1)}, u32[]{:S(2)}, u32[]{:S(2)}) %all-to-all-start.3) | async-done | bytes 3145760 | tf_op jit(solution)/shard_map/all_to_all | solution.py:274
  240.1 5.2 %couple.4 = (f32[8,128,128]{2,1,0:T(8,128)S(1)}, bf16[8,128,128]{2,1,0:T(8,128)(2,1)}, bf16[64,2,8,256]{3,2,1,0:T(8,128)(2,1)S(1)}) custom-call(f32[8,12]{1,0:T(8,128)S(1)} %copy-done.7, bf16[64,2,6,8,256]{4,3,2,1,0:T(8,128)(2,1)S(1)} %bitcast.60, bf16[8,128,1536]{2,1,0:T(8,128)(2,1)} %get-tuple-element.259.refs_2_, f32[8,128,128]{2,1,0:T(8,128)S(1)} %copy-done.2, ...), custom_call_target="tpu_custom_call" | custom-call | tf_op jit(solution)/shard_map/couple/pallas_call | solution.py:262
  246.1 18.2 %all_to_all.32 = bf16[128,8,256]{2,1,0:T(8,128)(2,1)} all-to-all(bf16[128,8,256]{2,1,0:T(8,128)(2,1)S(1)} %bitcast.62), channel_id=1, replica_groups=mesh['pairs'=128] {'pairs'}, dimensions={0} | all-to-all | bytes 1048576 | tf_op jit(solution)/shard_map/all_to_all | solution.py:274
  264.3 7.3 %pick_pieces.5 = bf16[128,48,256]{2,1,0:T(8,128)(2,1)} custom-call(s32[4,48,32]{2,1,0:T(8,128)} %bitcast.71, bf16[1024,256]{1,0:T(8,128)(2,1)} %bitcast.66), custom_call_target="tpu_custom_call" | custom-call | flops 3221225472 | bytes 3670016 | tf_op jit(solution)/shard_map/pick_pieces/pallas_call | solution.py:135
  271.5 4.5 %all-to-all-start.5 = ((bf16[128,48,256]{2,1,0:T(8,128)(2,1)}), bf16[128,48,256]{2,1,0:T(8,128)(2,1)S(1)}, u32[]{:S(2)}, u32[]{:S(2)}) async-start(bf16[128,48,256]{2,1,0:T(8,128)(2,1)} %pick_pieces.5), calls=%async_computation.5 | async-start | bytes 6291456 | tf_op jit(solution)/shard_map/all_to_all | solution.py:274
  276.1 22.2 %while.44 = (s32[]{:T(128)}, f32[8,128,128]{2,1,0:T(8,128)}, bf16[8,40,128,128]{3,2,1,0:T(8,128)(2,1)}, bf16[8,128,128]{2,1,0:T(8,128)(2,1)}, s32[]{:T(128)}, /*index=5*/s32[]{:T(128)}, s32[]{:T(128)}, s32[]{:T(128)}) while((s32[]{:T(128)}, f32[8,128,128]{2,1,0:T(8,128)}, bf16[8,40,128,128]{3,2,1,0:T(8,128)(2,1)}, ...), condition=%wide.region_5.0_spmd.clone, body=%wide.region_4.0_spmd.clone.sunk | while | flops 538181632 | bytes 5506708 | solution.py:317
  280.4 4.4 %fusion.103 = f32[8,128,128]{2,1,0:T(8,128)} fusion(bf16[8,40,128,128]{3,2,1,0:T(8,128)(2,1)} %get-tuple-element.479, s32[]{:T(128)S(6)} %select_n.29, f32[8,128,128]{2,1,0:T(8,128)} %get-tuple-element.470, bf16[8,128,128]{2,1,0:T(8,128)(2,1)} %get-tuple-element.480, pred[]{:T(512)S(6)} %compare.11), kind=kOutput, calls=%fused_computation.21.clone.1 | convolution fusion | flops 538181632 | bytes 5506560 | tf_op jit(solution)/shard_map/while/body/eval_jaxpr/rqad,rqbd->rab/dot_general | solution.py:313
  284.9 4.5 %fusion.103 = f32[8,128,128]{2,1,0:T(8,128)} fusion(bf16[8,40,128,128]{3,2,1,0:T(8,128)(2,1)} %get-tuple-element.479, s32[]{:T(128)S(6)} %select_n.29, f32[8,128,128]{2,1,0:T(8,128)} %get-tuple-element.470, bf16[8,128,128]{2,1,0:T(8,128)(2,1)} %get-tuple-element.480, pred[]{:T(512)S(6)} %compare.11), kind=kOutput, calls=%fused_computation.21.clone.1 | convolution fusion | flops 538181632 | bytes 5506560 | tf_op jit(solution)/shard_map/while/body/eval_jaxpr/rqad,rqbd->rab/dot_general | solution.py:313
  289.4 4.4 %fusion.103 = f32[8,128,128]{2,1,0:T(8,128)} fusion(bf16[8,40,128,128]{3,2,1,0:T(8,128)(2,1)} %get-tuple-element.479, s32[]{:T(128)S(6)} %select_n.29, f32[8,128,128]{2,1,0:T(8,128)} %get-tuple-element.470, bf16[8,128,128]{2,1,0:T(8,128)(2,1)} %get-tuple-element.480, pred[]{:T(512)S(6)} %compare.11), kind=kOutput, calls=%fused_computation.21.clone.1 | convolution fusion | flops 538181632 | bytes 5506560 | tf_op jit(solution)/shard_map/while/body/eval_jaxpr/rqad,rqbd->rab/dot_general | solution.py:313
  300.6 17.2 %all-to-all-done.5 = bf16[128,48,256]{2,1,0:T(8,128)(2,1)S(1)} async-done(((bf16[128,48,256]{2,1,0:T(8,128)(2,1)}), bf16[128,48,256]{2,1,0:T(8,128)(2,1)S(1)}, u32[]{:S(2)}, u32[]{:S(2)}) %all-to-all-start.5) | async-done | bytes 3145760 | tf_op jit(solution)/shard_map/all_to_all | solution.py:274
  320.9 5.3 %couple.5 = f32[8,128,128]{2,1,0:T(8,128)} custom-call(f32[8,12]{1,0:T(8,128)S(1)} %copy-done.7, bf16[64,2,6,8,256]{4,3,2,1,0:T(8,128)(2,1)S(1)} %bitcast.61, bf16[8,128,1536]{2,1,0:T(8,128)(2,1)} %get-tuple-element.259.refs_2_, f32[8,128,128]{2,1,0:T(8,128)S(1)} %copy-done.5, f32[8,128,128]{2,1,0:T(8,128)S(1)} %copy-done.6, f32[8,128,128]{2,1,0:T(8,128)S(1)} %copy-done.1), custom_call_target="tpu_custom_call" | custom-call | tf_op jit(solution)/shard_map/couple/pallas_call | solution.py:262
  (54 shorter events, 53.8 us)
Async XLA Ops:
  38.9 1.2 copy-start.9
  53.9 6.2 %copy-start.13 = (bf16[8,12]{1,0:T(8,128)(2,1)S(1)}, bf16[8,12]{1,0:T(8,128)(2,1)}, u32[]{:S(2)}) copy-start(bf16[8,12]{1,0:T(8,128)(2,1)} %param.23) | copy-start | bytes 580
  53.9 6.7 %copy-start.14 = (s32[8]{0:T(128)S(1)}, s32[8]{0:T(128)}, u32[]{:S(2)}) copy-start(s32[8]{0:T(128)} %count_ref.1) | copy-start | bytes 100
  53.9 98.4 %all-to-all-start.1 = ((bf16[128,48,640]{2,1,0:T(8,128)(2,1)}), bf16[128,48,640]{2,1,0:T(8,128)(2,1)}, u32[]{:S(2)}, u32[]{:S(2)}) async-start(bf16[128,48,640]{2,1,0:T(8,128)(2,1)} %pick_pieces.3), calls=%async_computation.1 | async-start | bytes 15728640 | tf_op jit(solution)/shard_map/all_to_all | solution.py:274
  60.8 18.5 %copy-start.8 = (bf16[8,128,128]{2,1,0:T(8,128)(2,1)S(1)}, bf16[8,128,128]{2,1,0:T(8,128)(2,1)}, u32[]{:S(2)}) copy-start(bf16[8,128,128]{2,1,0:T(8,128)(2,1)} %exchange_ref.1) | copy-start | bytes 786436
  60.8 18.5 %copy-start.10 = (f32[8,128,128]{2,1,0:T(8,128)S(1)}, f32[8,128,128]{2,1,0:T(8,128)}, u32[]{:S(2)}) copy-start(f32[8,128,128]{2,1,0:T(8,128)} %get-tuple-element.255.refs_3_) | copy-start | bytes 1572868
  60.8 18.5 %copy-start.11 = (f32[8,128]{1,0:T(8,128)S(1)}, f32[8,128]{1,0:T(8,128)}, u32[]{:S(2)}) copy-start(f32[8,128]{1,0:T(8,128)} %energy_ref.1) | copy-start | bytes 12292
  60.8 18.5 %copy-start.12 = (f32[8]{0:T(128)S(1)}, f32[8]{0:T(128)}, u32[]{:S(2)}) copy-start(f32[8]{0:T(128)} %occ_ref.1) | copy-start | bytes 100
  190.7 46.3 %all-to-all-start.3 = ((bf16[128,48,256]{2,1,0:T(8,128)(2,1)}), bf16[128,48,256]{2,1,0:T(8,128)(2,1)S(1)}, u32[]{:S(2)}, u32[]{:S(2)}) async-start(bf16[128,48,256]{2,1,0:T(8,128)(2,1)} %pick_pieces.4), calls=%async_computation.3 | async-start | bytes 6291456 | tf_op jit(solution)/shard_map/all_to_all | solution.py:274
  195.2 41.7 %copy-start.7 = (f32[8,12]{1,0:T(8,128)S(1)}, f32[8,12]{1,0:T(8,128)}, u32[]{:S(2)}) copy-start(f32[8,12]{1,0:T(8,128)} %convert_element_type.41.refs_0_) | copy-start | bytes 1156
  237.0 1.0 copy-start
  238.0 1.0 copy-start.2
  239.1 1.0 copy-start.3
  245.3 0.8 copy-start.4
  271.5 46.3 %all-to-all-start.5 = ((bf16[128,48,256]{2,1,0:T(8,128)(2,1)}), bf16[128,48,256]{2,1,0:T(8,128)(2,1)S(1)}, u32[]{:S(2)}, u32[]{:S(2)}) async-start(bf16[128,48,256]{2,1,0:T(8,128)(2,1)} %pick_pieces.5), calls=%async_computation.5 | async-start | bytes 6291456 | tf_op jit(solution)/shard_map/all_to_all | solution.py:274
  317.8 1.0 copy-start.1
  318.8 1.0 copy-start.5
  319.9 1.0 copy-start.6

commit v3 on v2

--- a/solution.py
+++ b/solution.py
@@ -11,6 +11,7 @@
 LEVEL_SHIFT = 0.3
 LANES = 128
 TURN = 32
+COUPLE_VMEM = 48 << 20
 F32 = jnp.float32
 BF16 = jnp.bfloat16
 NT = (((1,), (1,)), ((), ()))
@@ -30,7 +31,7 @@
 
 
 def store_pieces(stack, send_ref, first_lane):
-    chips, _, own, _ = send_ref.shape
+    chips, own, _ = send_ref.shape
     parts = stack[0].shape[0] // chips
     back = regroup(TURN, own, True)
     for start in range(0, chips, TURN):
@@ -45,17 +46,14 @@
         )
         pieces = jnp.dot(back, rows, preferred_element_type=F32).astype(BF16)
         pieces = pieces.reshape(TURN, own, parts * LANES)
-        for core in range(2):
-            send_ref[start : start + TURN, core, :, first_lane : first_lane + parts * LANES] = (
-                pieces
-            )
+        send_ref[start : start + TURN, :, first_lane : first_lane + parts * LANES] = pieces
 
 
 def start_kernel(
     count_ref, occ_ref, owner_ref, local_ref, basis_ref, exchange_ref, energy_ref,
     amp_ref, sent_ref, turned_ref, send_ref,
 ):
-    chips, _, own, width = send_ref.shape
+    chips, own, width = send_ref.shape
     domain, orbitals = basis_ref.shape[1:]
     row = lax.broadcasted_iota(jnp.int32, (orbitals, orbitals), 0)
     col = lax.broadcasted_iota(jnp.int32, (orbitals, orbitals), 1)
@@ -75,16 +73,14 @@
         turned_ref[p] = masked.T.astype(BF16)
         stack.append(jnp.concatenate([sent, masked.astype(BF16)], axis=0))
     store_pieces(stack, send_ref, 0)
-    half = owner_ref.shape[1] // 2
-    empty = jnp.zeros((own, LANES - 2 * half), F32)
-    for core in range(2):
-        mine = slice(core * half, (core + 1) * half)
-        asked = jnp.concatenate(
-            [owner_ref[:, mine].astype(F32), local_ref[:, mine].astype(F32), empty], axis=1
-        )
-        send_ref[:, core, :, width - LANES :] = jnp.broadcast_to(
-            asked.astype(BF16)[None], (chips, own, LANES)
-        )
+    partners = owner_ref.shape[1]
+    empty = jnp.zeros((own, LANES - 2 * partners), F32)
+    asked = jnp.concatenate(
+        [owner_ref[...].astype(F32), local_ref[...].astype(F32), empty], axis=1
+    )
+    send_ref[:, :, width - LANES :] = jnp.broadcast_to(
+        asked.astype(BF16)[None], (chips, own, LANES)
+    )
 
 
 def start(count, occ, owner, local, basis, exchange, energy, chips):
@@ -99,15 +95,15 @@
             jax.ShapeDtypeStruct((own, orbitals, orbitals), F32),
             jax.ShapeDtypeStruct((own, orbitals, orbitals), BF16),
             jax.ShapeDtypeStruct((own, orbitals, domain), BF16),
-            jax.ShapeDtypeStruct((chips, 2, own, width), BF16),
+            jax.ShapeDtypeStruct((chips, own, width), BF16),
         ],
         name="start",
     )(count, occ, owner, local, basis, exchange, energy)
 
 
-def pick_kernel(list_ref, table_ref, out_ref, onehot_ref):
+def pick_kernel(core_ref, list_ref, near_ref, mate_ref, out_ref, onehot_ref):
     half, group = list_ref.shape[1:]
-    rows, width = table_ref.shape
+    held, width = near_ref.shape
     lane = lax.broadcasted_iota(jnp.int32, (half, LANES), 1).astype(F32).astype(BF16)
     one, zero = jnp.bfloat16(1), jnp.bfloat16(0)
     at_once = 4
@@ -117,57 +113,66 @@
             tile_of = lax.shift_right_logical(wanted, 7).astype(F32).astype(BF16)
             lane_of = jnp.bitwise_and(wanted, LANES - 1).astype(F32).astype(BF16)
             hit = jnp.where(lane_of == lane, one, zero)
-            for tile in range(rows // LANES):
+            for tile in range(2 * held // LANES):
                 onehot_ref[
                     member * half : (member + 1) * half, tile * LANES : (tile + 1) * LANES
                 ] = jnp.where(tile_of == jnp.bfloat16(tile), hit, zero)
+        rows = slice(begin * half, (begin + at_once) * half)
         picked = jnp.dot(
-            onehot_ref[begin * half : (begin + at_once) * half],
-            table_ref[...],
-            preferred_element_type=F32,
-        )
-        out_ref[begin : begin + at_once] = picked.astype(BF16).reshape(at_once, half, width)
-
-
-def pick_pieces(lists, table, width):
+            onehot_ref[rows, :held], near_ref[...], preferred_element_type=F32
+        ) + jnp.dot(onehot_ref[rows, held:], mate_ref[...], preferred_element_type=F32)
+        out_ref[begin : begin + at_once, 0] = picked.astype(BF16).reshape(at_once, half, width)
+
+
+def pick_pieces(core, lists, near, mate, width):
     groups, half, group = lists.shape
-    rows = table.shape[0]
+    held = near.shape[0]
+    chips = groups * group // 2
+    halves = groups // 2
+    table = pl.BlockSpec((held, width), lambda g, core: (0, 0))
     return pl.pallas_call(
         pick_kernel,
-        grid=(groups,),
-        in_specs=[
-            pl.BlockSpec((1, half, group), lambda g: (g, 0, 0)),
-            pl.BlockSpec((rows, width), lambda g: (0, 0)),
-        ],
-        out_specs=pl.BlockSpec((group, half, width), lambda g: (g, 0, 0)),
-        out_shape=jax.ShapeDtypeStruct((groups * group, half, width), BF16),
-        scratch_shapes=[pltpu.VMEM((group * half, rows), BF16)],
+        grid_spec=pltpu.PrefetchScalarGridSpec(
+            num_scalar_prefetch=1,
+            grid=(groups,),
+            in_specs=[pl.BlockSpec((1, half, group), lambda g, core: (g, 0, 0)), table, table],
+            out_specs=pl.BlockSpec(
+                (group, 1, half, width),
+                lambda g, core: (
+                    lax.rem(g, halves),
+                    jnp.bitwise_xor(lax.div(g, halves), core[0]),
+                    0,
+                    0,
+                ),
+            ),
+            scratch_shapes=[pltpu.VMEM((group * half, 2 * held), BF16)],
+        ),
+        out_shape=jax.ShapeDtypeStruct((chips, 2, half, width), BF16),
         cost_estimate=pl.CostEstimate(
-            flops=2 * groups * group * half * rows * width,
-            bytes_accessed=2 * (rows * width + groups * group * half * width),
+            flops=4 * groups * group * half * held * width,
+            bytes_accessed=2 * (2 * held * width + groups * group * half * width),
             transcendentals=0,
         ),
         name="pick_pieces",
-    )(lists, table)
+    )(core, lists, near, mate)
 
 
 def couple_kernel(first, last, *refs):
     refs = list(refs)
-    weight_ref, arrived_hbm, margin_hbm = refs[:3]
-    amp_hbm, rest_hbm, div_hbm, out_ref = refs[3:7]
+    weight_ref, occ_ref, energy_ref, arrived_hbm, margin_hbm, known_hbm, out_ref = refs[:7]
     refs = refs[7:]
     if not last:
         sent_ref, send_ref = refs[:2]
         refs = refs[2:]
     if first:
         margin_ref, refs = refs[0], refs[1:]
-    other_ref, left_ref, held_ref, amp_ref, rest_ref, div_ref, sems = refs[:7]
+    other_ref, left_ref, held_ref, known_ref, sems = refs[:5]
     if first:
-        turned_ref, basis_ref, arrived_ref = held_ref, refs[7], refs[8]
+        turned_ref, basis_ref, arrived_ref = held_ref, refs[5], refs[6]
     else:
         margin_ref, arrived_ref = held_ref, arrived_hbm
     chips, _, steps, own, width = arrived_ref.shape
-    orbitals = amp_ref.shape[1]
+    orbitals = known_ref.shape[1]
     blocks = chips // TURN
     copies = []
     if first:
@@ -176,19 +181,15 @@
             copies.append(
                 pltpu.make_async_copy(arrived_hbm.at[rows], arrived_ref.at[rows], sems.at[i])
             )
-    for i, (source, target) in enumerate(
-        [(margin_hbm, held_ref), (amp_hbm, amp_ref), (rest_hbm, rest_ref), (div_hbm, div_ref)]
-    ):
-        copies.append(pltpu.make_async_copy(source, target, sems.at[blocks + i]))
-    landed = copies[:-4]
-    copies = copies[-4:]
-    for copy in landed + copies:
+    margin_copy = pltpu.make_async_copy(margin_hbm, held_ref, sems.at[blocks])
+    known_copy = pltpu.make_async_copy(known_hbm, known_ref, sems.at[blocks + 1])
+    for copy in copies + [margin_copy, known_copy]:
         copy.start()
     order = regroup(TURN, own, False)
     for block in range(blocks):
         begin = block * TURN
         if first:
-            landed[block].wait()
+            copies[block].wait()
         for step in range(steps):
             for core in range(2):
                 c = core * steps + step
@@ -204,7 +205,7 @@
                         basis_ref[p, place : place + TURN, c * LANES : (c + 1) * LANES] = part(
                             rows, i
                         )
-    copies[0].wait()
+    margin_copy.wait()
     for p in range(own):
         if first:
             margin_ref[p] = jnp.dot(
@@ -219,12 +220,13 @@
             left_ref[p, :, c * orbitals : (c + 1) * orbitals] = (left * weight_ref[p, c]).astype(
                 BF16
             )
-    for copy in copies[1:]:
-        copy.wait()
+    known_copy.wait()
     stack = []
     for p in range(own):
         coupled = lax.dot_general(left_ref[p], margin_ref[p], NT, preferred_element_type=F32)
-        amplitudes = amp_ref[p] - (rest_ref[p] + coupled) / div_ref[p]
+        energy = jnp.broadcast_to(energy_ref[p : p + 1, :], (orbitals, orbitals))
+        divisor = energy.T + energy - occ_ref[p] + LEVEL_SHIFT
+        amplitudes = known_ref[p] - coupled / divisor
         out_ref[p] = amplitudes
         if not last:
             sent = amplitudes.astype(BF16)
@@ -234,26 +236,25 @@
         store_pieces(stack, send_ref, 0)
 
 
-def couple(first, last, weights, arrived, margin, amplitudes, rest, divisor):
+def couple(first, last, weights, occ, energy, arrived, margin, known):
     chips, _, steps, own, width = arrived.shape
-    orbitals = amplitudes.shape[1]
+    orbitals = known.shape[1]
     vectors = pl.BlockSpec(memory_space=pltpu.VMEM)
     far = pl.BlockSpec(memory_space=pltpu.HBM)
+    scalars = pl.BlockSpec(memory_space=pltpu.SMEM)
     all_columns = 2 * steps * orbitals
-    out_shape = [jax.ShapeDtypeStruct(amplitudes.shape, F32)]
+    out_shape = [jax.ShapeDtypeStruct(known.shape, F32)]
     scratch_shapes = [
         pltpu.VMEM((own, 2 * steps, orbitals, orbitals), BF16),
         pltpu.VMEM((own, orbitals, all_columns), BF16),
         pltpu.VMEM(margin.shape, BF16),
-        pltpu.VMEM(amplitudes.shape, F32),
-        pltpu.VMEM(amplitudes.shape, F32),
-        pltpu.VMEM(amplitudes.shape, F32),
-        pltpu.SemaphoreType.DMA((chips // TURN + 4,)),
+        pltpu.VMEM(known.shape, F32),
+        pltpu.SemaphoreType.DMA((chips // TURN + 2,)),
     ]
     if not last:
         out_shape += [
-            jax.ShapeDtypeStruct(amplitudes.shape, BF16),
-            jax.ShapeDtypeStruct((chips, 2, own, orbitals // chips * LANES), BF16),
+            jax.ShapeDtypeStruct(known.shape, BF16),
+            jax.ShapeDtypeStruct((chips, own, orbitals // chips * LANES), BF16),
         ]
     if first:
         out_shape.append(jax.ShapeDtypeStruct((own, orbitals, all_columns), BF16))
@@ -261,17 +262,19 @@
         scratch_shapes.append(pltpu.VMEM(arrived.shape, BF16))
     return pl.pallas_call(
         functools.partial(couple_kernel, first, last),
-        in_specs=[pl.BlockSpec(memory_space=pltpu.SMEM), far if first else vectors] + [far] * 4,
+        in_specs=[scalars, scalars, vectors, far if first else vectors, far, far],
         out_specs=[vectors] * len(out_shape),
         out_shape=out_shape,
         scratch_shapes=scratch_shapes,
-        compiler_params=None if first else pltpu.CompilerParams(vmem_limit_bytes=48 << 20),
+        compiler_params=None if first else pltpu.CompilerParams(vmem_limit_bytes=COUPLE_VMEM),
         name="couple",
-    )(weights, arrived, margin, amplitudes, rest, divisor)
-
-
-def swap(values):
-    return lax.all_to_all(values, "pairs", split_axis=0, concat_axis=0, tiled=True)
+    )(weights, occ, energy, arrived, margin, known)
+
+
+def swap(values, groups=None):
+    return lax.all_to_all(
+        values, "pairs", split_axis=0, concat_axis=0, tiled=True, axis_index_groups=groups
+    )
 
 
 def shards(
@@ -291,8 +294,11 @@
     fitted = ladder_factor.shape[1]
     partners = partner_owner.shape[1]
     half = own * partners // 2
-    rows = devices * own
+    held = chips * own
     group = 32
+    core = lax.rem(lax.axis_index("pairs"), 2).astype(jnp.int32)
+    same_core = [list(range(k, devices, 2)) for k in range(2)]
+    mates = [(i, i + 1 - 2 * (i % 2)) for i in range(devices)]
     columns = lax.broadcasted_iota(jnp.int32, (own, orbitals), 1)
     live_cols = (columns < pno_count[:, None]).astype(F32)
     energy_sum = pno_energy[:, :, None] + pno_energy[:, None, :] - occ_energy[:, None, None]
@@ -324,25 +330,33 @@
     lists = None
     for iteration in range(ITERS):
         first, last = iteration == 0, iteration == ITERS - 1
-        held = swap(send.reshape(devices, own, send.shape[-1]))
+        near = swap(send, same_core)
+        mate = lax.ppermute(near, "pairs", mates)
         width = 2 * LANES
         if first:
-            width = held.shape[-1] - LANES
-            names = held[:, :, width : width + partners].astype(jnp.int32)
-            lists = names[:, :, : partners // 2] * own + names[:, :, partners // 2 :]
+            width = near.shape[-1] - LANES
+            names = slice(width, width + 2 * partners)
+            asked = jnp.concatenate([near[:, :, names], mate[:, :, names]], axis=0)
+            asked = asked.astype(jnp.int32).reshape(devices, own, 2, 2, partners // 2)
+            asked = jnp.where(core == 0, asked[:, :, :, 0], asked[:, :, :, 1])
+            owner, local = asked[:, :, 0], asked[:, :, 1]
+            lists = jnp.bitwise_xor(owner % 2, core) * held + owner // 2 * own + local
             lists = lists.reshape(devices // group, group, own, partners // 2)
             lists = jnp.transpose(lists, (0, 3, 2, 1)).reshape(devices // group, half, group)
-        arrived = swap(pick_pieces(lists, held.reshape(rows, held.shape[-1]), width))
+        tables = [table.reshape(held, table.shape[-1]) for table in (near, mate)]
+        pieces = pick_pieces(core.reshape(1), lists, *tables, width)
+        arrived = swap(pieces.reshape(devices, half, width))
         rest = driving + energy_sum * amplitudes + ladder_of(sent)
+        known = amplitudes - rest / divisor
         results = couple(
             first,
             last,
             weights,
+            occ_energy,
+            pno_energy,
             arrived.reshape(chips, 2, partners // 2, own, width),
             margin,
-            amplitudes,
-            rest,
-            divisor,
+            known,
         )
         amplitudes = results[0]
         if not last:

time: 328 us -> 317 us (0.966)
  blocking collectives: 74.9 us -> 56.6 us
  starting transfers between devices: 15.2 us -> 19.8 us
  waiting for transfers between devices: 106 us -> 110 us
    all_to_all x3, blocking collectives: 74.9 us -> 56.6 us  [swap(): lax.all_to_all(values, 'pairs', split_axis=0, concat_axis=0, tiled=True,...]
    ppermute x0 -> x3, starting transfers between devices: none -> 7.02 us  [shards(): mate = lax.ppermute(near, 'pairs', mates)]
    add x4 -> x0, other arithmetic: 6 us -> none  [the longest x2 4.69 us: shards(): rest = driving + energy_sum * amplitudes + ladder_of(sent)]
    sub x0 -> x3, other arithmetic: none -> 5.86 us  [shards(): known = amplitudes - rest / divisor]
    ppermute x0 -> x3, waiting for transfers between devices: none -> 4.08 us  [shards(): mate = lax.ppermute(near, 'pairs', mates)]
    unnamed x31 -> x36, local copies, waits for them, and re-layouts: 7.27 us -> 4.31 us
  transfers between devices with their start and end apart: 3 -> 6, of which waited for: 3 -> 6; matrix products, arithmetic and copies ran while one was open for 21% -> 22% of each run, Pallas kernels for 0% -> 0%
where the time goes in v3:
time: 317 us; the launch traced here: 316 us
  waiting for transfers between devices  110 us (35%)
  matrix products  62.7 us (20%)
  blocking collectives  56.6 us (18%)
  Pallas kernels  53.7 us (17%)
  starting transfers between devices  19.8 us (6%)
  other arithmetic  6.83 us (2%)
  local copies, waits for them, and re-layouts  5.46 us (2%)
    all_to_all x3, waiting for transfers between devices, swap(): lax.all_to_all(values, 'pairs', split_axis=0, concat_axis=0, tiled=True,...  106 us
    dot_general x15, matrix products, add_group(): jnp.einsum('rqad,rqbd->rab', ladder_half, factors, preferred_element_type...  62.7 us
    all_to_all x3, blocking collectives, swap(): lax.all_to_all(values, 'pairs', split_axis=0, concat_axis=0, tiled=True,...  56.6 us
    pallas_call x3, Pallas kernels, pick_pieces(): pl.pallas_call(pick_kernel, grid_spec=pltpu.PrefetchScalarGridSpec(num_sc...  29.3 us
    pallas_call x3, Pallas kernels, couple(): pl.pallas_call(functools.partial(couple_kernel, first, last), in_specs=[s...  21.7 us
    all_to_all x3, starting transfers between devices, swap(): lax.all_to_all(values, 'pairs', split_axis=0, concat_axis=0, tiled=True,...  12.8 us
    ppermute x3, starting transfers between devices, shards(): mate = lax.ppermute(near, 'pairs', mates)  7.02 us
  transfers between devices with their start and end apart: 6, of which 6 were waited for; matrix products, arithmetic and copies ran while one was open for 22% of the time, Pallas kernels for 0%

profile of v3, /device:TPU:1, one launch (start us, length us, event | category | flops | bytes accessed | tf_op | source)
XLA Modules:
  0.0 316.0 jit_solution(2930790526234228410)
XLA Ops:
  2.7 26.5 %all_to_all.30 = bf16[64,8,768]{2,1,0:T(8,128)(2,1)S(1)} all-to-all(bf16[64,8,768]{2,1,0:T(8,128)(2,1)} %get-tuple-element.253), channel_id=1, replica_groups={{0,2,4,6,8,10,12,14,16,18,20,22,24,26,28,30,32,34,36,38,40,42,44,46,48,..., dimensions={0} | all-to-all | bytes 1572864 | tf_op jit(solution)/shard_map/all_to_all | solution.py:275
  34.9 14.3 %pick_pieces.3 = bf16[64,2,48,640]{3,2,1,0:T(8,128)(2,1)} custom-call(s32[1]{0:T(128)} %bitcast.core_ref, s32[4,48,32]{2,1,0:T(8,128)} %bitcast.85, bf16[512,768]{1,0:T(8,128)(2,1)} %bitcast.80, bf16[512,768]{1,0:T(8,128)(2,1)} %bitcast.88), custom_call_target="tpu_custom_call" | custom-call | flops 8053063680 | bytes 9175040 | tf_op jit(solution)/shard_map/pick_pieces/pallas_call | solution.py:133
  49.2 5.1 %all-to-all-start.1 = ((bf16[128,48,640]{2,1,0:T(8,128)(2,1)}), bf16[128,48,640]{2,1,0:T(8,128)(2,1)}, u32[]{:S(2)}, u32[]{:S(2)}) async-start(bf16[128,48,640]{2,1,0:T(8,128)(2,1)} %bitcast.77), calls=%async_computation.1 | async-start | bytes 15728640 | tf_op jit(solution)/shard_map/all_to_all | solution.py:275
  55.0 18.5 %while.42 = (s32[]{:T(128)}, f32[8,128,128]{2,1,0:T(8,128)S(1)}, bf16[8,40,128,128]{3,2,1,0:T(8,128)(2,1)}, bf16[8,128,128]{2,1,0:T(8,128)(2,1)S(1)}, s32[]{:T(128)}, /*index=5*/s32[]{:T(128)}, s32[]{:T(128)}, s32[]{:T(128)}) while((s32[]{:T(128)}, f32[8,128,128]{2,1,0:T(8,128)S(1)}, bf16[8,40,128,128]{3,2,1,0:T(8,128)(2,1)}, ...), condition=%wide.region_1.2_spmd.clone, body=%wide.region_0.1_spmd.clone.sunk | while | flops 538181632 | bytes 5506700 | solution.py:323
  74.7 71.8 %all-to-all-done.1 = bf16[128,48,640]{2,1,0:T(8,128)(2,1)} async-done(((bf16[128,48,640]{2,1,0:T(8,128)(2,1)}), bf16[128,48,640]{2,1,0:T(8,128)(2,1)}, u32[]{:S(2)}, u32[]{:S(2)}) %all-to-all-start.1) | async-done | bytes 7864352 | tf_op jit(solution)/shard_map/all_to_all | solution.py:275
  146.5 11.2 %couple.3 = (f32[8,128,128]{2,1,0:T(8,128)}, bf16[8,128,128]{2,1,0:T(8,128)(2,1)}, bf16[64,8,256]{2,1,0:T(8,128)(2,1)}, bf16[8,128,1536]{2,1,0:T(8,128)(2,1)}) custom-call(f32[8,12]{1,0:T(8,128)} %convert_element_type.42.refs_0_, f32[8]{0:T(128)} %refs_1_.5, f32[8,128]{1,0:T(8,128)} %refs_2_.5, bf16[64,2,6,8,640]{4,3,2,1,0:T(8,128)(2,1)} %bitcast.9.refs_3_, ...), custom_call_target="tpu_custom_call" | custom-call | tf_op jit(solution)/shard_map/couple/pallas_call | solution.py:263
  157.7 16.9 %all_to_all.31 = bf16[64,8,256]{2,1,0:T(8,128)(2,1)S(1)} all-to-all(bf16[64,8,256]{2,1,0:T(8,128)(2,1)} %get-tuple-element.258), channel_id=1, replica_groups={{0,2,4,6,8,10,12,14,16,18,20,22,24,26,28,30,32,34,36,38,40,42,44,46,48,..., dimensions={0} | all-to-all | bytes 524288 | tf_op jit(solution)/shard_map/all_to_all | solution.py:275
  178.8 7.5 %pick_pieces.4 = bf16[64,2,48,256]{3,2,1,0:T(8,128)(2,1)} custom-call(s32[1]{0:T(128)} %bitcast.core_ref, s32[4,48,32]{2,1,0:T(8,128)} %bitcast.86, bf16[512,256]{1,0:T(8,128)(2,1)} %bitcast.82, bf16[512,256]{1,0:T(8,128)(2,1)} %bitcast.90), custom_call_target="tpu_custom_call" | custom-call | flops 3221225472 | bytes 3670016 | tf_op jit(solution)/shard_map/pick_pieces/pallas_call | solution.py:133
  190.2 22.2 %while.43 = (s32[]{:T(128)}, f32[8,128,128]{2,1,0:T(8,128)}, bf16[8,40,128,128]{3,2,1,0:T(8,128)(2,1)}, bf16[8,128,128]{2,1,0:T(8,128)(2,1)}, s32[]{:T(128)}, /*index=5*/s32[]{:T(128)}, s32[]{:T(128)}, s32[]{:T(128)}) while((s32[]{:T(128)}, f32[8,128,128]{2,1,0:T(8,128)}, bf16[8,40,128,128]{3,2,1,0:T(8,128)(2,1)}, ...), condition=%wide.region_3.4_spmd.clone, body=%wide.region_2.3_spmd.clone.sunk | while | flops 538181632 | bytes 5506700 | solution.py:323
  194.6 4.5 %fusion.108 = f32[8,128,128]{2,1,0:T(8,128)} fusion(bf16[8,40,128,128]{3,2,1,0:T(8,128)(2,1)} %get-tuple-element.455, s32[]{:T(128)S(6)} %select_n.78, f32[8,128,128]{2,1,0:T(8,128)} %get-tuple-element.446, bf16[8,128,128]{2,1,0:T(8,128)(2,1)} %get-tuple-element.456, pred[]{:T(512)S(6)} %compare.16), kind=kOutput, calls=%fused_computation.13.clone.1 | convolution fusion | flops 538181632 | bytes 5506560 | tf_op jit(solution)/shard_map/while/body/eval_jaxpr/rqad,rqbd->rab/dot_general | solution.py:319
  199.1 4.4 %fusion.108 = f32[8,128,128]{2,1,0:T(8,128)} fusion(bf16[8,40,128,128]{3,2,1,0:T(8,128)(2,1)} %get-tuple-element.455, s32[]{:T(128)S(6)} %select_n.78, f32[8,128,128]{2,1,0:T(8,128)} %get-tuple-element.446, bf16[8,128,128]{2,1,0:T(8,128)(2,1)} %get-tuple-element.456, pred[]{:T(512)S(6)} %compare.16), kind=kOutput, calls=%fused_computation.13.clone.1 | convolution fusion | flops 538181632 | bytes 5506560 | tf_op jit(solution)/shard_map/while/body/eval_jaxpr/rqad,rqbd->rab/dot_general | solution.py:319
  203.5 4.5 %fusion.108 = f32[8,128,128]{2,1,0:T(8,128)} fusion(bf16[8,40,128,128]{3,2,1,0:T(8,128)(2,1)} %get-tuple-element.455, s32[]{:T(128)S(6)} %select_n.78, f32[8,128,128]{2,1,0:T(8,128)} %get-tuple-element.446, bf16[8,128,128]{2,1,0:T(8,128)(2,1)} %get-tuple-element.456, pred[]{:T(512)S(6)} %compare.16), kind=kOutput, calls=%fused_computation.13.clone.1 | convolution fusion | flops 538181632 | bytes 5506560 | tf_op jit(solution)/shard_map/while/body/eval_jaxpr/rqad,rqbd->rab/dot_general | solution.py:319
  207.9 4.4 %fusion.108 = f32[8,128,128]{2,1,0:T(8,128)} fusion(bf16[8,40,128,128]{3,2,1,0:T(8,128)(2,1)} %get-tuple-element.455, s32[]{:T(128)S(6)} %select_n.78, f32[8,128,128]{2,1,0:T(8,128)} %get-tuple-element.446, bf16[8,128,128]{2,1,0:T(8,128)(2,1)} %get-tuple-element.456, pred[]{:T(512)S(6)} %compare.16), kind=kOutput, calls=%fused_computation.13.clone.1 | convolution fusion | flops 538181632 | bytes 5506560 | tf_op jit(solution)/shard_map/while/body/eval_jaxpr/rqad,rqbd->rab/dot_general | solution.py:319
  214.7 17.2 %all-to-all-done.3 = bf16[128,48,256]{2,1,0:T(8,128)(2,1)S(1)} async-done(((bf16[128,48,256]{2,1,0:T(8,128)(2,1)}), bf16[128,48,256]{2,1,0:T(8,128)(2,1)S(1)}, u32[]{:S(2)}, u32[]{:S(2)}) %all-to-all-start.3) | async-done | bytes 3145760 | tf_op jit(solution)/shard_map/all_to_all | solution.py:275
  232.9 5.2 %couple.4 = (f32[8,128,128]{2,1,0:T(8,128)S(1)}, bf16[8,128,128]{2,1,0:T(8,128)(2,1)}, bf16[64,8,256]{2,1,0:T(8,128)(2,1)S(1)}) custom-call(f32[8,12]{1,0:T(8,128)S(1)} %copy-done.5, f32[8]{0:T(128)S(1)} %copy-done.7, f32[8,128]{1,0:T(8,128)S(1)} %copy-done.4, bf16[64,2,6,8,256]{4,3,2,1,0:T(8,128)(2,1)S(1)} %bitcast.76, ...), custom_call_target="tpu_custom_call" | custom-call | tf_op jit(solution)/shard_map/couple/pallas_call | solution.py:263
  238.9 13.2 %all_to_all.32 = bf16[64,8,256]{2,1,0:T(8,128)(2,1)S(1)} all-to-all(bf16[64,8,256]{2,1,0:T(8,128)(2,1)S(1)} %get-tuple-element.263), channel_id=1, replica_groups={{0,2,4,6,8,10,12,14,16,18,20,22,24,26,28,30,32,34,36,38,40,42,44,46,48,..., dimensions={0} | all-to-all | bytes 524288 | tf_op jit(solution)/shard_map/all_to_all | solution.py:275
  256.4 7.5 %pick_pieces.5 = bf16[64,2,48,256]{3,2,1,0:T(8,128)(2,1)} custom-call(s32[1]{0:T(128)} %bitcast.core_ref, s32[4,48,32]{2,1,0:T(8,128)} %bitcast.87, bf16[512,256]{1,0:T(8,128)(2,1)} %bitcast.81, bf16[512,256]{1,0:T(8,128)(2,1)} %bitcast.89), custom_call_target="tpu_custom_call" | custom-call | flops 3221225472 | bytes 3670016 | tf_op jit(solution)/shard_map/pick_pieces/pallas_call | solution.py:133
  267.7 22.3 %while.44 = (s32[]{:T(128)}, f32[8,128,128]{2,1,0:T(8,128)}, bf16[8,40,128,128]{3,2,1,0:T(8,128)(2,1)}, bf16[8,128,128]{2,1,0:T(8,128)(2,1)}, s32[]{:T(128)}, /*index=5*/s32[]{:T(128)}, s32[]{:T(128)}, s32[]{:T(128)}) while((s32[]{:T(128)}, f32[8,128,128]{2,1,0:T(8,128)}, bf16[8,40,128,128]{3,2,1,0:T(8,128)(2,1)}, ...), condition=%wide.region_5.6_spmd.clone, body=%wide.region_4.5_spmd.clone.sunk | while | flops 538181632 | bytes 5506700 | solution.py:323
  272.2 4.5 %fusion.113 = f32[8,128,128]{2,1,0:T(8,128)} fusion(bf16[8,40,128,128]{3,2,1,0:T(8,128)(2,1)} %get-tuple-element.479, s32[]{:T(128)S(6)} %select_n.79, f32[8,128,128]{2,1,0:T(8,128)} %get-tuple-element.470, bf16[8,128,128]{2,1,0:T(8,128)(2,1)} %get-tuple-element.480, pred[]{:T(512)S(6)} %compare.17), kind=kOutput, calls=%fused_computation.21.clone.1 | convolution fusion | flops 538181632 | bytes 5506560 | tf_op jit(solution)/shard_map/while/body/eval_jaxpr/rqad,rqbd->rab/dot_general | solution.py:319
  276.7 4.4 %fusion.113 = f32[8,128,128]{2,1,0:T(8,128)} fusion(bf16[8,40,128,128]{3,2,1,0:T(8,128)(2,1)} %get-tuple-element.479, s32[]{:T(128)S(6)} %select_n.79, f32[8,128,128]{2,1,0:T(8,128)} %get-tuple-element.470, bf16[8,128,128]{2,1,0:T(8,128)(2,1)} %get-tuple-element.480, pred[]{:T(512)S(6)} %compare.17), kind=kOutput, calls=%fused_computation.21.clone.1 | convolution fusion | flops 538181632 | bytes 5506560 | tf_op jit(solution)/shard_map/while/body/eval_jaxpr/rqad,rqbd->rab/dot_general | solution.py:319
  281.1 4.5 %fusion.113 = f32[8,128,128]{2,1,0:T(8,128)} fusion(bf16[8,40,128,128]{3,2,1,0:T(8,128)(2,1)} %get-tuple-element.479, s32[]{:T(128)S(6)} %select_n.79, f32[8,128,128]{2,1,0:T(8,128)} %get-tuple-element.470, bf16[8,128,128]{2,1,0:T(8,128)(2,1)} %get-tuple-element.480, pred[]{:T(512)S(6)} %compare.17), kind=kOutput, calls=%fused_computation.21.clone.1 | convolution fusion | flops 538181632 | bytes 5506560 | tf_op jit(solution)/shard_map/while/body/eval_jaxpr/rqad,rqbd->rab/dot_general | solution.py:319
  285.6 4.4 %fusion.113 = f32[8,128,128]{2,1,0:T(8,128)} fusion(bf16[8,40,128,128]{3,2,1,0:T(8,128)(2,1)} %get-tuple-element.479, s32[]{:T(128)S(6)} %select_n.79, f32[8,128,128]{2,1,0:T(8,128)} %get-tuple-element.470, bf16[8,128,128]{2,1,0:T(8,128)(2,1)} %get-tuple-element.480, pred[]{:T(512)S(6)} %compare.17), kind=kOutput, calls=%fused_computation.21.clone.1 | convolution fusion | flops 538181632 | bytes 5506560 | tf_op jit(solution)/shard_map/while/body/eval_jaxpr/rqad,rqbd->rab/dot_general | solution.py:319
  292.4 17.1 %all-to-all-done.5 = bf16[128,48,256]{2,1,0:T(8,128)(2,1)S(1)} async-done(((bf16[128,48,256]{2,1,0:T(8,128)(2,1)}), bf16[128,48,256]{2,1,0:T(8,128)(2,1)S(1)}, u32[]{:S(2)}, u32[]{:S(2)}) %all-to-all-start.5) | async-done | bytes 3145760 | tf_op jit(solution)/shard_map/all_to_all | solution.py:275
  310.5 5.3 %couple.5 = f32[8,128,128]{2,1,0:T(8,128)} custom-call(f32[8,12]{1,0:T(8,128)S(1)} %copy-done.5, f32[8]{0:T(128)S(1)} %copy-done.7, f32[8,128]{1,0:T(8,128)S(1)} %copy-done.4, bf16[64,2,6,8,256]{4,3,2,1,0:T(8,128)(2,1)S(1)} %bitcast.75, bf16[8,128,1536]{2,1,0:T(8,128)(2,1)} %get-tuple-element.259.refs_4_, f32[8,128,128]{2,1,0:T(8,128)S(1)} %copy-done), custom_call_target="tpu_custom_call" | custom-call | tf_op jit(solution)/shard_map/couple/pallas_call | solution.py:263
  (71 shorter events, 60.9 us)
Async XLA Ops:
  29.3 5.6 %copy-start.9 = (bf16[64,8,768]{2,1,0:T(8,128)(2,1)}, bf16[64,8,768]{2,1,0:T(8,128)(2,1)S(1)}, u32[]{:S(2)}) copy-start(bf16[64,8,768]{2,1,0:T(8,128)(2,1)S(1)} %all_to_all.30) | copy-start | bytes 2359300
  29.3 4.3 %collective-permute-start = (bf16[64,8,768]{2,1,0:T(8,128)(2,1)S(1)}, bf16[64,8,768]{2,1,0:T(8,128)(2,1)S(1)}, u32[]{:S(2)}, u32[]{:S(2)}) collective-permute-start(bf16[64,8,768]{2,1,0:T(8,128)(2,1)S(1)} %all_to_all.30), channel_id=1, source_target_pairs={{0,1},{1,0},{2,3},{3,2},{4,5},{5,4},{6,7},{7,6},{8,9},{9,8},{10,11... | collective-permute-start | bytes 2359304 | tf_op jit(solution)/shard_map/ppermute | solution.py:334
  33.6 1.4 copy-start.13
  49.2 5.1 %copy-start.14 = (bf16[8,12]{1,0:T(8,128)(2,1)S(1)}, bf16[8,12]{1,0:T(8,128)(2,1)}, u32[]{:S(2)}) copy-start(bf16[8,12]{1,0:T(8,128)(2,1)} %param.23) | copy-start | bytes 580
  49.2 5.7 %copy-start.15 = (s32[8]{0:T(128)S(1)}, s32[8]{0:T(128)}, u32[]{:S(2)}) copy-start(s32[8]{0:T(128)} %count_ref.1) | copy-start | bytes 100
  49.2 97.3 %all-to-all-start.1 = ((bf16[128,48,640]{2,1,0:T(8,128)(2,1)}), bf16[128,48,640]{2,1,0:T(8,128)(2,1)}, u32[]{:S(2)}, u32[]{:S(2)}) async-start(bf16[128,48,640]{2,1,0:T(8,128)(2,1)} %bitcast.77), calls=%async_computation.1 | async-start | bytes 15728640 | tf_op jit(solution)/shard_map/all_to_all | solution.py:275
  55.0 18.5 %copy-start.3 = (f32[8,128]{1,0:T(8,128)S(1)}, f32[8,128]{1,0:T(8,128)}, u32[]{:S(2)}) copy-start(f32[8,128]{1,0:T(8,128)} %refs_2_.5) | copy-start | bytes 12292
  55.0 18.5 %copy-start.6 = (f32[8]{0:T(128)S(1)}, f32[8]{0:T(128)}, u32[]{:S(2)}) copy-start(f32[8]{0:T(128)} %refs_1_.5) | copy-start | bytes 100
  55.0 18.5 %copy-start.8 = (bf16[8,128,128]{2,1,0:T(8,128)(2,1)S(1)}, bf16[8,128,128]{2,1,0:T(8,128)(2,1)}, u32[]{:S(2)}) copy-start(bf16[8,128,128]{2,1,0:T(8,128)(2,1)} %exchange_ref.1) | copy-start | bytes 786436
  55.0 18.5 %copy-start.10 = (f32[8,128,128]{2,1,0:T(8,128)S(1)}, f32[8,128,128]{2,1,0:T(8,128)}, u32[]{:S(2)}) copy-start(f32[8,128,128]{2,1,0:T(8,128)} %get-tuple-element.255) | copy-start | bytes 1572868
  174.6 3.5 %copy-start.12 = (bf16[64,8,256]{2,1,0:T(8,128)(2,1)}, bf16[64,8,256]{2,1,0:T(8,128)(2,1)S(1)}, u32[]{:S(2)}) copy-start(bf16[64,8,256]{2,1,0:T(8,128)(2,1)S(1)} %all_to_all.31) | copy-start | bytes 786436
  174.6 3.5 %collective-permute-start.1 = (bf16[64,8,256]{2,1,0:T(8,128)(2,1)S(1)}, bf16[64,8,256]{2,1,0:T(8,128)(2,1)S(1)}, u32[]{:S(2)}, u32[]{:S(2)}) collective-permute-start(bf16[64,8,256]{2,1,0:T(8,128)(2,1)S(1)} %all_to_all.31), channel_id=1, source_target_pairs={{0,1},{1,0},{2,3},{3,2},{4,5},{5,4},{6,7},{7,6},{8,9},{9,8},{10,11... | collective-permute-start | bytes 786440 | tf_op jit(solution)/shard_map/ppermute | solution.py:334
  178.1 0.7 copy-start.17
  186.3 45.6 %all-to-all-start.3 = ((bf16[128,48,256]{2,1,0:T(8,128)(2,1)}), bf16[128,48,256]{2,1,0:T(8,128)(2,1)S(1)}, u32[]{:S(2)}, u32[]{:S(2)}) async-start(bf16[128,48,256]{2,1,0:T(8,128)(2,1)} %bitcast.79), calls=%async_computation.3 | async-start | bytes 6291456 | tf_op jit(solution)/shard_map/all_to_all | solution.py:275
  190.1 22.2 %copy-start.4 = (f32[8,128]{1,0:T(8,128)S(1)}, f32[8,128]{1,0:T(8,128)}, u32[]{:S(2)}) copy-start(f32[8,128]{1,0:T(8,128)} %refs_2_.5) | copy-start | bytes 12292
  190.1 22.2 %copy-start.7 = (f32[8]{0:T(128)S(1)}, f32[8]{0:T(128)}, u32[]{:S(2)}) copy-start(f32[8]{0:T(128)} %refs_1_.5) | copy-start | bytes 100
  190.2 41.7 %copy-start.5 = (f32[8,12]{1,0:T(8,128)S(1)}, f32[8,12]{1,0:T(8,128)}, u32[]{:S(2)}) copy-start(f32[8,12]{1,0:T(8,128)} %convert_element_type.42.refs_0_) | copy-start | bytes 1156
  231.9 1.0 copy-start.1
  238.1 0.8 copy-start.2
  252.2 3.5 %copy-start.11 = (bf16[64,8,256]{2,1,0:T(8,128)(2,1)}, bf16[64,8,256]{2,1,0:T(8,128)(2,1)S(1)}, u32[]{:S(2)}) copy-start(bf16[64,8,256]{2,1,0:T(8,128)(2,1)S(1)} %all_to_all.32) | copy-start | bytes 786436
  252.2 3.5 %collective-permute-start.2 = (bf16[64,8,256]{2,1,0:T(8,128)(2,1)S(1)}, bf16[64,8,256]{2,1,0:T(8,128)(2,1)S(1)}, u32[]{:S(2)}, u32[]{:S(2)}) collective-permute-start(bf16[64,8,256]{2,1,0:T(8,128)(2,1)S(1)} %all_to_all.32), channel_id=1, source_target_pairs={{0,1},{1,0},{2,3},{3,2},{4,5},{5,4},{6,7},{7,6},{8,9},{9,8},{10,11... | collective-permute-start | bytes 786440 | tf_op jit(solution)/shard_map/ppermute | solution.py:334
  255.7 0.7 copy-start.16
  263.9 45.6 %all-to-all-start.5 = ((bf16[128,48,256]{2,1,0:T(8,128)(2,1)}), bf16[128,48,256]{2,1,0:T(8,128)(2,1)S(1)}, u32[]{:S(2)}, u32[]{:S(2)}) async-start(bf16[128,48,256]{2,1,0:T(8,128)(2,1)} %bitcast.78), calls=%async_computation.5 | async-start | bytes 6291456 | tf_op jit(solution)/shard_map/all_to_all | solution.py:275
  309.5 1.0 copy-start

commit v4 on v3

--- a/solution.py
+++ b/solution.py
@@ -10,19 +10,18 @@
 ITERS = 3
 LEVEL_SHIFT = 0.3
 LANES = 128
-TURN = 32
-COUPLE_VMEM = 48 << 20
+TURN = 16
+COUPLE_VMEM = 51 << 20
 F32 = jnp.float32
 BF16 = jnp.bfloat16
 NT = (((1,), (1,)), ((), ()))
 
 
-def regroup(major, minor, turned):
+def regroup(major, minor):
     size = major * minor
-    row = lax.broadcasted_iota(jnp.int32, (size, size), 0)
-    col = lax.broadcasted_iota(jnp.int32, (size, size), 1)
-    to, source = (col, row) if turned else (row, col)
-    hit = source == lax.rem(to, major) * minor + lax.div(to, major)
+    to = lax.broadcasted_iota(jnp.int32, (size, size), 0)
+    source = lax.broadcasted_iota(jnp.int32, (size, size), 1)
+    hit = source == lax.rem(to, minor) * major + lax.div(to, minor)
     return jnp.where(hit, 1.0, 0.0).astype(BF16)
 
 
@@ -33,7 +32,7 @@
 def store_pieces(stack, send_ref, first_lane):
     chips, own, _ = send_ref.shape
     parts = stack[0].shape[0] // chips
-    back = regroup(TURN, own, True)
+    back = regroup(TURN, own)
     for start in range(0, chips, TURN):
         rows = jnp.concatenate(
             [
@@ -159,44 +158,41 @@
 
 def couple_kernel(first, last, *refs):
     refs = list(refs)
-    weight_ref, occ_ref, energy_ref, arrived_hbm, margin_hbm, known_hbm, out_ref = refs[:7]
+    weight_ref, occ_ref, energy_ref, arrived_hbm, margin_hbm, known_hbm, out_hbm = refs[:7]
     refs = refs[7:]
     if not last:
         sent_ref, send_ref = refs[:2]
         refs = refs[2:]
     if first:
         margin_ref, refs = refs[0], refs[1:]
-    other_ref, left_ref, held_ref, known_ref, sems = refs[:5]
+    other_ref, left_ref, held_ref, known_ref, arrived_ref, sems = refs[:6]
     if first:
-        turned_ref, basis_ref, arrived_ref = held_ref, refs[5], refs[6]
+        turned_ref, basis_ref = held_ref, refs[6]
     else:
-        margin_ref, arrived_ref = held_ref, arrived_hbm
+        margin_ref = held_ref
     chips, _, steps, own, width = arrived_ref.shape
     orbitals = known_ref.shape[1]
     blocks = chips // TURN
     copies = []
-    if first:
-        for i in range(blocks):
-            rows = pl.ds(i * TURN, TURN)
-            copies.append(
-                pltpu.make_async_copy(arrived_hbm.at[rows], arrived_ref.at[rows], sems.at[i])
-            )
+    for i in range(blocks):
+        rows = pl.ds(i * TURN, TURN)
+        copies.append(
+            pltpu.make_async_copy(arrived_hbm.at[rows], arrived_ref.at[rows], sems.at[i])
+        )
     margin_copy = pltpu.make_async_copy(margin_hbm, held_ref, sems.at[blocks])
     known_copy = pltpu.make_async_copy(known_hbm, known_ref, sems.at[blocks + 1])
     for copy in copies + [margin_copy, known_copy]:
         copy.start()
-    order = regroup(TURN, own, False)
     for block in range(blocks):
         begin = block * TURN
-        if first:
-            copies[block].wait()
+        copies[block].wait()
         for step in range(steps):
             for core in range(2):
                 c = core * steps + step
-                arrived = arrived_ref[begin : begin + TURN, core, step].reshape(TURN * own, width)
-                moved = jnp.dot(order, arrived, preferred_element_type=F32).astype(BF16)
+                arrived = arrived_ref[begin : begin + TURN, core, step]
+                moved = jnp.transpose(arrived, (1, 0, 2))
                 for p in range(own):
-                    rows = moved[p * TURN : (p + 1) * TURN]
+                    rows = moved[p]
                     for i in range(orbitals // chips):
                         place = i * chips + begin
                         other_ref[p, c, place : place + TURN, :] = part(rows, i)
@@ -221,19 +217,24 @@
                 BF16
             )
     known_copy.wait()
-    stack = []
+    stack, leaving = [], []
     for p in range(own):
         coupled = lax.dot_general(left_ref[p], margin_ref[p], NT, preferred_element_type=F32)
         energy = jnp.broadcast_to(energy_ref[p : p + 1, :], (orbitals, orbitals))
         divisor = energy.T + energy - occ_ref[p] + LEVEL_SHIFT
         amplitudes = known_ref[p] - coupled / divisor
-        out_ref[p] = amplitudes
+        known_ref[p] = amplitudes
+        leave = pltpu.make_async_copy(known_ref.at[p], out_hbm.at[p], sems.at[blocks + 2 + p])
+        leave.start()
+        leaving.append(leave)
         if not last:
             sent = amplitudes.astype(BF16)
             sent_ref[p] = sent
             stack.append(sent)
     if not last:
         store_pieces(stack, send_ref, 0)
+    for leave in leaving:
+        leave.wait()
 
 
 def couple(first, last, weights, occ, energy, arrived, margin, known):
@@ -249,7 +250,8 @@
         pltpu.VMEM((own, orbitals, all_columns), BF16),
         pltpu.VMEM(margin.shape, BF16),
         pltpu.VMEM(known.shape, F32),
-        pltpu.SemaphoreType.DMA((chips // TURN + 2,)),
+        pltpu.VMEM(arrived.shape, BF16),
+        pltpu.SemaphoreType.DMA((chips // TURN + 2 + own,)),
     ]
     if not last:
         out_shape += [
@@ -259,12 +261,12 @@
     if first:
         out_shape.append(jax.ShapeDtypeStruct((own, orbitals, all_columns), BF16))
         scratch_shapes.append(pltpu.VMEM((own, margin.shape[2], all_columns), BF16))
-        scratch_shapes.append(pltpu.VMEM(arrived.shape, BF16))
     return pl.pallas_call(
         functools.partial(couple_kernel, first, last),
-        in_specs=[scalars, scalars, vectors, far if first else vectors, far, far],
-        out_specs=[vectors] * len(out_shape),
+        in_specs=[scalars, scalars, vectors, far, far, far],
+        out_specs=[far] + [vectors] * (len(out_shape) - 1),
         out_shape=out_shape,
+        input_output_aliases={5: 0},
         scratch_shapes=scratch_shapes,
         compiler_params=None if first else pltpu.CompilerParams(vmem_limit_bytes=COUPLE_VMEM),
         name="couple",

time: 317 us -> 319 us (level)
  waiting for transfers between devices: 110 us -> 120 us
  matrix products: 62.7 us -> 54.8 us
  Pallas kernels: 53.7 us -> 57 us
  other arithmetic: 6.83 us -> 3.64 us
    all_to_all x3, waiting for transfers between devices: 106 us -> 116 us  [swap(): lax.all_to_all(values, 'pairs', split_axis=0, concat_axis=0, tiled=True,...]
    dot_general x15, matrix products: 62.7 us -> 54.8 us  [add_group(): jnp.einsum('rqad,rqbd->rab', ladder_half, factors, preferred_element_type...]
    pallas_call x3, Pallas kernels: 21.7 us -> 25.1 us  [couple(): pl.pallas_call(functools.partial(couple_kernel, first, last), in_specs=[s...]
    sub x3, other arithmetic: 5.86 us -> 2.67 us  [shards(): known = amplitudes - rest / divisor]
  transfers between devices with their start and end apart: 6 -> 6, of which waited for: 6 -> 6; matrix products, arithmetic and copies ran while one was open for 22% -> 18% of each run, Pallas kernels for 0% -> 0%
where the time goes in v4:
time: 319 us; the launch traced here: 318 us
  waiting for transfers between devices  120 us (38%)
  Pallas kernels  57 us (18%)
  blocking collectives  56.6 us (18%)
  matrix products  54.8 us (17%)
  starting transfers between devices  22 us (7%)
  other arithmetic  3.64 us (1%)
    all_to_all x3, waiting for transfers between devices, swap(): lax.all_to_all(values, 'pairs', split_axis=0, concat_axis=0, tiled=True,...  116 us
    all_to_all x3, blocking collectives, swap(): lax.all_to_all(values, 'pairs', split_axis=0, concat_axis=0, tiled=True,...  56.6 us
    dot_general x15, matrix products, add_group(): jnp.einsum('rqad,rqbd->rab', ladder_half, factors, preferred_element_type...  54.8 us
    pallas_call x3, Pallas kernels, pick_pieces(): pl.pallas_call(pick_kernel, grid_spec=pltpu.PrefetchScalarGridSpec(num_sc...  29.2 us
    pallas_call x3, Pallas kernels, couple(): pl.pallas_call(functools.partial(couple_kernel, first, last), in_specs=[s...  25.1 us
    all_to_all x3, starting transfers between devices, swap(): lax.all_to_all(values, 'pairs', split_axis=0, concat_axis=0, tiled=True,...  15 us
    ppermute x3, starting transfers between devices, shards(): mate = lax.ppermute(near, 'pairs', mates)  7.03 us
  transfers between devices with their start and end apart: 6, of which 6 were waited for; matrix products, arithmetic and copies ran while one was open for 18% of the time, Pallas kernels for 0%

profile of v4, /device:TPU:1, one launch (start us, length us, event | category | flops | bytes accessed | tf_op | source)
XLA Modules:
  0.0 318.1 jit_solution(16442157812039707235)
XLA Ops:
  2.7 26.5 %all_to_all.30 = bf16[64,8,768]{2,1,0:T(8,128)(2,1)S(1)} all-to-all(bf16[64,8,768]{2,1,0:T(8,128)(2,1)} %get-tuple-element.253), channel_id=1, replica_groups={{0,2,4,6,8,10,12,14,16,18,20,22,24,26,28,30,32,34,36,38,40,42,44,46,48,..., dimensions={0} | all-to-all | bytes 1572864 | tf_op jit(solution)/shard_map/all_to_all | solution.py:277
  34.9 14.3 %pick_pieces.3 = bf16[64,2,48,640]{3,2,1,0:T(8,128)(2,1)} custom-call(s32[1]{0:T(128)} %bitcast.core_ref, s32[4,48,32]{2,1,0:T(8,128)} %bitcast.83, bf16[512,768]{1,0:T(8,128)(2,1)} %bitcast.78, bf16[512,768]{1,0:T(8,128)(2,1)} %bitcast.86), custom_call_target="tpu_custom_call" | custom-call | flops 8053063680 | bytes 9175040 | tf_op jit(solution)/shard_map/pick_pieces/pallas_call | solution.py:132
  49.2 5.1 %all-to-all-start.1 = ((bf16[128,48,640]{2,1,0:T(8,128)(2,1)}), bf16[128,48,640]{2,1,0:T(8,128)(2,1)}, u32[]{:S(2)}, u32[]{:S(2)}) async-start(bf16[128,48,640]{2,1,0:T(8,128)(2,1)} %bitcast.75), calls=%async_computation.1 | async-start | bytes 15728640 | tf_op jit(solution)/shard_map/all_to_all | solution.py:277
  55.0 18.5 %while.42 = (s32[]{:T(128)}, f32[8,128,128]{2,1,0:T(8,128)S(1)}, bf16[8,40,128,128]{3,2,1,0:T(8,128)(2,1)}, bf16[8,128,128]{2,1,0:T(8,128)(2,1)S(1)}, s32[]{:T(128)}, /*index=5*/s32[]{:T(128)}, s32[]{:T(128)}, s32[]{:T(128)}) while((s32[]{:T(128)}, f32[8,128,128]{2,1,0:T(8,128)S(1)}, bf16[8,40,128,128]{3,2,1,0:T(8,128)(2,1)}, ...), condition=%wide.region_1.2_spmd.clone, body=%wide.region_0.1_spmd.clone.sunk | while | flops 538181632 | bytes 5506700 | solution.py:325
  55.0 3.7 %fusion.103 = f32[8,128,128]{2,1,0:T(8,128)S(1)} fusion(bf16[8,40,128,128]{3,2,1,0:T(8,128)(2,1)} %get-tuple-element.431, s32[]{:T(128)S(6)} %select_n.77, f32[8,128,128]{2,1,0:T(8,128)S(1)} %get-tuple-element.422, bf16[8,128,128]{2,1,0:T(8,128)(2,1)S(1)} %get-tuple-element.432, pred[]{:T(512)S(6)} %compare.15), kind=kOutput, calls=%fused_computation.5.clone.1 | convolution fusion | flops 538181632 | bytes 5506560 | tf_op jit(solution)/shard_map/while/body/eval_jaxpr/rqad,rqbd->rab/dot_general | solution.py:321
  58.7 3.6 %fusion.103 = f32[8,128,128]{2,1,0:T(8,128)S(1)} fusion(bf16[8,40,128,128]{3,2,1,0:T(8,128)(2,1)} %get-tuple-element.431, s32[]{:T(128)S(6)} %select_n.77, f32[8,128,128]{2,1,0:T(8,128)S(1)} %get-tuple-element.422, bf16[8,128,128]{2,1,0:T(8,128)(2,1)S(1)} %get-tuple-element.432, pred[]{:T(512)S(6)} %compare.15), kind=kOutput, calls=%fused_computation.5.clone.1 | convolution fusion | flops 538181632 | bytes 5506560 | tf_op jit(solution)/shard_map/while/body/eval_jaxpr/rqad,rqbd->rab/dot_general | solution.py:321
  62.4 3.7 %fusion.103 = f32[8,128,128]{2,1,0:T(8,128)S(1)} fusion(bf16[8,40,128,128]{3,2,1,0:T(8,128)(2,1)} %get-tuple-element.431, s32[]{:T(128)S(6)} %select_n.77, f32[8,128,128]{2,1,0:T(8,128)S(1)} %get-tuple-element.422, bf16[8,128,128]{2,1,0:T(8,128)(2,1)S(1)} %get-tuple-element.432, pred[]{:T(512)S(6)} %compare.15), kind=kOutput, calls=%fused_computation.5.clone.1 | convolution fusion | flops 538181632 | bytes 5506560 | tf_op jit(solution)/shard_map/while/body/eval_jaxpr/rqad,rqbd->rab/dot_general | solution.py:321
  74.6 71.8 %all-to-all-done.1 = bf16[128,48,640]{2,1,0:T(8,128)(2,1)} async-done(((bf16[128,48,640]{2,1,0:T(8,128)(2,1)}), bf16[128,48,640]{2,1,0:T(8,128)(2,1)}, u32[]{:S(2)}, u32[]{:S(2)}) %all-to-all-start.1) | async-done | bytes 7864352 | tf_op jit(solution)/shard_map/all_to_all | solution.py:277
  146.5 10.7 %couple.3 = (f32[8,128,128]{2,1,0:T(8,128)}, bf16[8,128,128]{2,1,0:T(8,128)(2,1)S(1)}, bf16[64,8,256]{2,1,0:T(8,128)(2,1)}, bf16[8,128,1536]{2,1,0:T(8,128)(2,1)}) custom-call(f32[8,12]{1,0:T(8,128)} %convert_element_type.42.refs_0_, f32[8]{0:T(128)} %refs_1_.5, f32[8,128]{1,0:T(8,128)} %refs_2_.5, ...), custom_call_target="tpu_custom_call", output_to_operand_aliasing={{0}: (5, {})} | custom-call | tf_op jit(solution)/shard_map/couple/pallas_call | solution.py:264
  157.1 16.9 %all_to_all.31 = bf16[64,8,256]{2,1,0:T(8,128)(2,1)S(1)} all-to-all(bf16[64,8,256]{2,1,0:T(8,128)(2,1)} %get-tuple-element.258), channel_id=1, replica_groups={{0,2,4,6,8,10,12,14,16,18,20,22,24,26,28,30,32,34,36,38,40,42,44,46,48,..., dimensions={0} | all-to-all | bytes 524288 | tf_op jit(solution)/shard_map/all_to_all | solution.py:277
  178.2 7.5 %pick_pieces.4 = bf16[64,2,48,256]{3,2,1,0:T(8,128)(2,1)} custom-call(s32[1]{0:T(128)} %bitcast.core_ref, s32[4,48,32]{2,1,0:T(8,128)} %bitcast.84, bf16[512,256]{1,0:T(8,128)(2,1)} %bitcast.80, bf16[512,256]{1,0:T(8,128)(2,1)} %bitcast.88), custom_call_target="tpu_custom_call" | custom-call | flops 3221225472 | bytes 3670016 | tf_op jit(solution)/shard_map/pick_pieces/pallas_call | solution.py:132
  185.7 4.9 %all-to-all-start.3 = ((bf16[128,48,256]{2,1,0:T(8,128)(2,1)}), bf16[128,48,256]{2,1,0:T(8,128)(2,1)}, u32[]{:S(2)}, u32[]{:S(2)}) async-start(bf16[128,48,256]{2,1,0:T(8,128)(2,1)} %bitcast.77), calls=%async_computation.3 | async-start | bytes 6291456 | tf_op jit(solution)/shard_map/all_to_all | solution.py:277
  190.7 18.4 %while.43 = (s32[]{:T(128)}, f32[8,128,128]{2,1,0:T(8,128)S(1)}, bf16[8,40,128,128]{3,2,1,0:T(8,128)(2,1)}, bf16[8,128,128]{2,1,0:T(8,128)(2,1)S(1)}, s32[]{:T(128)}, /*index=5*/s32[]{:T(128)}, s32[]{:T(128)}, s32[]{:T(128)}) while((s32[]{:T(128)}, f32[8,128,128]{2,1,0:T(8,128)S(1)}, bf16[8,40,128,128]{3,2,1,0:T(8,128)(2,1)}, ...), condition=%wide.region_3.4_spmd.clone, body=%wide.region_2.3_spmd.clone.sunk | while | flops 538181632 | bytes 5506700 | solution.py:325
  190.7 3.7 %fusion.108 = f32[8,128,128]{2,1,0:T(8,128)S(1)} fusion(bf16[8,40,128,128]{3,2,1,0:T(8,128)(2,1)} %get-tuple-element.455, s32[]{:T(128)S(6)} %select_n.78, f32[8,128,128]{2,1,0:T(8,128)S(1)} %get-tuple-element.446, bf16[8,128,128]{2,1,0:T(8,128)(2,1)S(1)} %get-tuple-element.456, pred[]{:T(512)S(6)} %compare.16), kind=kOutput, calls=%fused_computation.13.clone.1 | convolution fusion | flops 538181632 | bytes 5506560 | tf_op jit(solution)/shard_map/while/body/eval_jaxpr/rqad,rqbd->rab/dot_general | solution.py:321
  198.1 3.6 %fusion.108 = f32[8,128,128]{2,1,0:T(8,128)S(1)} fusion(bf16[8,40,128,128]{3,2,1,0:T(8,128)(2,1)} %get-tuple-element.455, s32[]{:T(128)S(6)} %select_n.78, f32[8,128,128]{2,1,0:T(8,128)S(1)} %get-tuple-element.446, bf16[8,128,128]{2,1,0:T(8,128)(2,1)S(1)} %get-tuple-element.456, pred[]{:T(512)S(6)} %compare.16), kind=kOutput, calls=%fused_computation.13.clone.1 | convolution fusion | flops 538181632 | bytes 5506560 | tf_op jit(solution)/shard_map/while/body/eval_jaxpr/rqad,rqbd->rab/dot_general | solution.py:321
  209.5 22.6 %all-to-all-done.3 = bf16[128,48,256]{2,1,0:T(8,128)(2,1)} async-done(((bf16[128,48,256]{2,1,0:T(8,128)(2,1)}), bf16[128,48,256]{2,1,0:T(8,128)(2,1)}, u32[]{:S(2)}, u32[]{:S(2)}) %all-to-all-start.3) | async-done | bytes 3145760 | tf_op jit(solution)/shard_map/all_to_all | solution.py:277
  232.1 8.2 %couple.4 = (f32[8,128,128]{2,1,0:T(8,128)S(1)}, bf16[8,128,128]{2,1,0:T(8,128)(2,1)S(1)}, bf16[64,8,256]{2,1,0:T(8,128)(2,1)S(1)}) custom-call(f32[8,12]{1,0:T(8,128)S(1)} %copy-done.2, f32[8]{0:T(128)S(1)} %copy-done.4, f32[8,128]{1,0:T(8,128)S(1)} %copy-done.1, bf16[64,2,6,8,256]{4,3,2,1,0:T(8,128)(2,1)} %bitcast.13.refs_3_, ...), custom_call_target="tpu_custom_call", output_to_operand_aliasing={{0}: (5, {})} | custom-call | tf_op jit(solution)/shard_map/couple/pallas_call | solution.py:264
  240.3 13.2 %all_to_all.32 = bf16[64,8,256]{2,1,0:T(8,128)(2,1)S(1)} all-to-all(bf16[64,8,256]{2,1,0:T(8,128)(2,1)S(1)} %get-tuple-element.263), channel_id=1, replica_groups={{0,2,4,6,8,10,12,14,16,18,20,22,24,26,28,30,32,34,36,38,40,42,44,46,48,..., dimensions={0} | all-to-all | bytes 524288 | tf_op jit(solution)/shard_map/all_to_all | solution.py:277
  257.8 7.5 %pick_pieces.5 = bf16[64,2,48,256]{3,2,1,0:T(8,128)(2,1)} custom-call(s32[1]{0:T(128)} %bitcast.core_ref, s32[4,48,32]{2,1,0:T(8,128)} %bitcast.85, bf16[512,256]{1,0:T(8,128)(2,1)} %bitcast.79, bf16[512,256]{1,0:T(8,128)(2,1)} %bitcast.87), custom_call_target="tpu_custom_call" | custom-call | flops 3221225472 | bytes 3670016 | tf_op jit(solution)/shard_map/pick_pieces/pallas_call | solution.py:132
  265.2 4.9 %all-to-all-start.5 = ((bf16[128,48,256]{2,1,0:T(8,128)(2,1)}), bf16[128,48,256]{2,1,0:T(8,128)(2,1)}, u32[]{:S(2)}, u32[]{:S(2)}) async-start(bf16[128,48,256]{2,1,0:T(8,128)(2,1)} %bitcast.76), calls=%async_computation.5 | async-start | bytes 6291456 | tf_op jit(solution)/shard_map/all_to_all | solution.py:277
  270.2 18.3 %while.44 = (s32[]{:T(128)}, f32[8,128,128]{2,1,0:T(8,128)S(1)}, bf16[8,40,128,128]{3,2,1,0:T(8,128)(2,1)}, bf16[8,128,128]{2,1,0:T(8,128)(2,1)S(1)}, s32[]{:T(128)}, /*index=5*/s32[]{:T(128)}, s32[]{:T(128)}, s32[]{:T(128)}) while((s32[]{:T(128)}, f32[8,128,128]{2,1,0:T(8,128)S(1)}, bf16[8,40,128,128]{3,2,1,0:T(8,128)(2,1)}, ...), condition=%wide.region_5.6_spmd.clone, body=%wide.region_4.5_spmd.clone.sunk | while | flops 538181632 | bytes 5506700 | solution.py:325
  270.2 3.6 %fusion.113 = f32[8,128,128]{2,1,0:T(8,128)S(1)} fusion(bf16[8,40,128,128]{3,2,1,0:T(8,128)(2,1)} %get-tuple-element.479, s32[]{:T(128)S(6)} %select_n.79, f32[8,128,128]{2,1,0:T(8,128)S(1)} %get-tuple-element.470, bf16[8,128,128]{2,1,0:T(8,128)(2,1)S(1)} %get-tuple-element.480, pred[]{:T(512)S(6)} %compare.17), kind=kOutput, calls=%fused_computation.21.clone.1 | convolution fusion | flops 538181632 | bytes 5506560 | tf_op jit(solution)/shard_map/while/body/eval_jaxpr/rqad,rqbd->rab/dot_general | solution.py:321
  289.7 21.9 %all-to-all-done.5 = bf16[128,48,256]{2,1,0:T(8,128)(2,1)} async-done(((bf16[128,48,256]{2,1,0:T(8,128)(2,1)}), bf16[128,48,256]{2,1,0:T(8,128)(2,1)}, u32[]{:S(2)}, u32[]{:S(2)}) %all-to-all-start.5) | async-done | bytes 3145760 | tf_op jit(solution)/shard_map/all_to_all | solution.py:277
  311.7 6.2 %couple.5 = f32[8,128,128]{2,1,0:T(8,128)} custom-call(f32[8,12]{1,0:T(8,128)S(1)} %copy-done.2, f32[8]{0:T(128)S(1)} %copy-done.4, f32[8,128]{1,0:T(8,128)S(1)} %copy-done.1, bf16[64,2,6,8,256]{4,3,2,1,0:T(8,128)(2,1)} %bitcast.17.refs_3_, bf16[8,128,1536]{2,1,0:T(8,128)(2,1)} %get-tuple-element.259.refs_4_, ...), custom_call_target="tpu_custom_call", output_to_operand_aliasing={{}: (5, {})} | custom-call | tf_op jit(solution)/shard_map/couple/pallas_call | solution.py:264
  (67 shorter events, 52.9 us)
Async XLA Ops:
  29.3 5.6 %copy-start.7 = (bf16[64,8,768]{2,1,0:T(8,128)(2,1)}, bf16[64,8,768]{2,1,0:T(8,128)(2,1)S(1)}, u32[]{:S(2)}) copy-start(bf16[64,8,768]{2,1,0:T(8,128)(2,1)S(1)} %all_to_all.30) | copy-start | bytes 2359300
  29.3 4.3 %collective-permute-start = (bf16[64,8,768]{2,1,0:T(8,128)(2,1)S(1)}, bf16[64,8,768]{2,1,0:T(8,128)(2,1)S(1)}, u32[]{:S(2)}, u32[]{:S(2)}) collective-permute-start(bf16[64,8,768]{2,1,0:T(8,128)(2,1)S(1)} %all_to_all.30), channel_id=1, source_target_pairs={{0,1},{1,0},{2,3},{3,2},{4,5},{5,4},{6,7},{7,6},{8,9},{9,8},{10,11... | collective-permute-start | bytes 2359304 | tf_op jit(solution)/shard_map/ppermute | solution.py:336
  33.5 1.4 copy-start.11
  49.2 5.1 %copy-start.12 = (bf16[8,12]{1,0:T(8,128)(2,1)S(1)}, bf16[8,12]{1,0:T(8,128)(2,1)}, u32[]{:S(2)}) copy-start(bf16[8,12]{1,0:T(8,128)(2,1)} %param.23) | copy-start | bytes 580
  49.2 5.7 %copy-start.13 = (s32[8]{0:T(128)S(1)}, s32[8]{0:T(128)}, u32[]{:S(2)}) copy-start(s32[8]{0:T(128)} %count_ref.1) | copy-start | bytes 100
  49.2 97.3 %all-to-all-start.1 = ((bf16[128,48,640]{2,1,0:T(8,128)(2,1)}), bf16[128,48,640]{2,1,0:T(8,128)(2,1)}, u32[]{:S(2)}, u32[]{:S(2)}) async-start(bf16[128,48,640]{2,1,0:T(8,128)(2,1)} %bitcast.75), calls=%async_computation.1 | async-start | bytes 15728640 | tf_op jit(solution)/shard_map/all_to_all | solution.py:277
  55.0 18.5 %copy-start = (f32[8,128]{1,0:T(8,128)S(1)}, f32[8,128]{1,0:T(8,128)}, u32[]{:S(2)}) copy-start(f32[8,128]{1,0:T(8,128)} %refs_2_.5) | copy-start | bytes 12292
  55.0 18.5 %copy-start.3 = (f32[8]{0:T(128)S(1)}, f32[8]{0:T(128)}, u32[]{:S(2)}) copy-start(f32[8]{0:T(128)} %refs_1_.5) | copy-start | bytes 100
  55.0 18.5 %copy-start.6 = (bf16[8,128,128]{2,1,0:T(8,128)(2,1)S(1)}, bf16[8,128,128]{2,1,0:T(8,128)(2,1)}, u32[]{:S(2)}) copy-start(bf16[8,128,128]{2,1,0:T(8,128)(2,1)} %exchange_ref.1) | copy-start | bytes 786436
  55.0 18.5 %copy-start.8 = (f32[8,128,128]{2,1,0:T(8,128)S(1)}, f32[8,128,128]{2,1,0:T(8,128)}, u32[]{:S(2)}) copy-start(f32[8,128,128]{2,1,0:T(8,128)} %get-tuple-element.255) | copy-start | bytes 1572868
  174.0 3.5 %copy-start.10 = (bf16[64,8,256]{2,1,0:T(8,128)(2,1)}, bf16[64,8,256]{2,1,0:T(8,128)(2,1)S(1)}, u32[]{:S(2)}) copy-start(bf16[64,8,256]{2,1,0:T(8,128)(2,1)S(1)} %all_to_all.31) | copy-start | bytes 786436
  174.0 3.5 %collective-permute-start.1 = (bf16[64,8,256]{2,1,0:T(8,128)(2,1)S(1)}, bf16[64,8,256]{2,1,0:T(8,128)(2,1)S(1)}, u32[]{:S(2)}, u32[]{:S(2)}) collective-permute-start(bf16[64,8,256]{2,1,0:T(8,128)(2,1)S(1)} %all_to_all.31), channel_id=1, source_target_pairs={{0,1},{1,0},{2,3},{3,2},{4,5},{5,4},{6,7},{7,6},{8,9},{9,8},{10,11... | collective-permute-start | bytes 786440 | tf_op jit(solution)/shard_map/ppermute | solution.py:336
  177.5 0.7 copy-start.15
  185.7 46.4 %all-to-all-start.3 = ((bf16[128,48,256]{2,1,0:T(8,128)(2,1)}), bf16[128,48,256]{2,1,0:T(8,128)(2,1)}, u32[]{:S(2)}, u32[]{:S(2)}) async-start(bf16[128,48,256]{2,1,0:T(8,128)(2,1)} %bitcast.77), calls=%async_computation.3 | async-start | bytes 6291456 | tf_op jit(solution)/shard_map/all_to_all | solution.py:277
  190.6 18.5 %copy-start.1 = (f32[8,128]{1,0:T(8,128)S(1)}, f32[8,128]{1,0:T(8,128)}, u32[]{:S(2)}) copy-start(f32[8,128]{1,0:T(8,128)} %refs_2_.5) | copy-start | bytes 12292
  190.6 18.5 %copy-start.4 = (f32[8]{0:T(128)S(1)}, f32[8]{0:T(128)}, u32[]{:S(2)}) copy-start(f32[8]{0:T(128)} %refs_1_.5) | copy-start | bytes 100
  190.6 18.5 %copy-start.5 = (f32[8,128,128]{2,1,0:T(8,128)S(1)}, f32[8,128,128]{2,1,0:T(8,128)}, u32[]{:S(2)}) copy-start(f32[8,128,128]{2,1,0:T(8,128)} %get-tuple-element.260) | copy-start | bytes 1572868
  190.7 41.4 %copy-start.2 = (f32[8,12]{1,0:T(8,128)S(1)}, f32[8,12]{1,0:T(8,128)}, u32[]{:S(2)}) copy-start(f32[8,12]{1,0:T(8,128)} %convert_element_type.42.refs_0_) | copy-start | bytes 1156
  253.6 3.5 %copy-start.9 = (bf16[64,8,256]{2,1,0:T(8,128)(2,1)}, bf16[64,8,256]{2,1,0:T(8,128)(2,1)S(1)}, u32[]{:S(2)}) copy-start(bf16[64,8,256]{2,1,0:T(8,128)(2,1)S(1)} %all_to_all.32) | copy-start | bytes 786436
  253.6 3.5 %collective-permute-start.2 = (bf16[64,8,256]{2,1,0:T(8,128)(2,1)S(1)}, bf16[64,8,256]{2,1,0:T(8,128)(2,1)S(1)}, u32[]{:S(2)}, u32[]{:S(2)}) collective-permute-start(bf16[64,8,256]{2,1,0:T(8,128)(2,1)S(1)} %all_to_all.32), channel_id=1, source_target_pairs={{0,1},{1,0},{2,3},{3,2},{4,5},{5,4},{6,7},{7,6},{8,9},{9,8},{10,11... | collective-permute-start | bytes 786440 | tf_op jit(solution)/shard_map/ppermute | solution.py:336
  257.1 0.7 copy-start.14
  265.2 46.4 %all-to-all-start.5 = ((bf16[128,48,256]{2,1,0:T(8,128)(2,1)}), bf16[128,48,256]{2,1,0:T(8,128)(2,1)}, u32[]{:S(2)}, u32[]{:S(2)}) async-start(bf16[128,48,256]{2,1,0:T(8,128)(2,1)} %bitcast.76), calls=%async_computation.5 | async-start | bytes 6291456 | tf_op jit(solution)/shard_map/all_to_all | solution.py:277

commit v5 on v4

--- a/solution.py
+++ b/solution.py
@@ -11,7 +11,7 @@
 LEVEL_SHIFT = 0.3
 LANES = 128
 TURN = 16
-COUPLE_VMEM = 51 << 20
+COUPLE_VMEM = 48 << 20
 F32 = jnp.float32
 BF16 = jnp.bfloat16
 NT = (((1,), (1,)), ((), ()))
@@ -165,27 +165,29 @@
         refs = refs[2:]
     if first:
         margin_ref, refs = refs[0], refs[1:]
-    other_ref, left_ref, held_ref, known_ref, arrived_ref, sems = refs[:6]
+    other_ref, left_ref, held_ref, known_ref, sems = refs[:5]
     if first:
-        turned_ref, basis_ref = held_ref, refs[6]
+        turned_ref, basis_ref, arrived_ref = held_ref, refs[5], refs[6]
     else:
-        margin_ref = held_ref
+        margin_ref, arrived_ref = held_ref, arrived_hbm
     chips, _, steps, own, width = arrived_ref.shape
     orbitals = known_ref.shape[1]
     blocks = chips // TURN
     copies = []
-    for i in range(blocks):
-        rows = pl.ds(i * TURN, TURN)
-        copies.append(
-            pltpu.make_async_copy(arrived_hbm.at[rows], arrived_ref.at[rows], sems.at[i])
-        )
+    if first:
+        for i in range(blocks):
+            rows = pl.ds(i * TURN, TURN)
+            copies.append(
+                pltpu.make_async_copy(arrived_hbm.at[rows], arrived_ref.at[rows], sems.at[i])
+            )
     margin_copy = pltpu.make_async_copy(margin_hbm, held_ref, sems.at[blocks])
     known_copy = pltpu.make_async_copy(known_hbm, known_ref, sems.at[blocks + 1])
     for copy in copies + [margin_copy, known_copy]:
         copy.start()
     for block in range(blocks):
         begin = block * TURN
-        copies[block].wait()
+        if first:
+            copies[block].wait()
         for step in range(steps):
             for core in range(2):
                 c = core * steps + step
@@ -250,7 +252,6 @@
         pltpu.VMEM((own, orbitals, all_columns), BF16),
         pltpu.VMEM(margin.shape, BF16),
         pltpu.VMEM(known.shape, F32),
-        pltpu.VMEM(arrived.shape, BF16),
         pltpu.SemaphoreType.DMA((chips // TURN + 2 + own,)),
     ]
     if not last:
@@ -261,9 +262,10 @@
     if first:
         out_shape.append(jax.ShapeDtypeStruct((own, orbitals, all_columns), BF16))
         scratch_shapes.append(pltpu.VMEM((own, margin.shape[2], all_columns), BF16))
+        scratch_shapes.append(pltpu.VMEM(arrived.shape, BF16))
     return pl.pallas_call(
         functools.partial(couple_kernel, first, last),
-        in_specs=[scalars, scalars, vectors, far, far, far],
+        in_specs=[scalars, scalars, vectors, far if first else vectors, far, far],
         out_specs=[far] + [vectors] * (len(out_shape) - 1),
         out_shape=out_shape,
         input_output_aliases={5: 0},

time: 319 us -> 318 us (level)
  waiting for transfers between devices: 120 us -> 110 us
  matrix products: 54.8 us -> 63 us
  other arithmetic: 3.64 us -> 6.83 us
    all_to_all x3, waiting for transfers between devices: 116 us -> 106 us  [swap(): lax.all_to_all(values, 'pairs', split_axis=0, concat_axis=0, tiled=True,...]
    dot_general x15, matrix products: 54.8 us -> 63 us  [add_group(): jnp.einsum('rqad,rqbd->rab', ladder_half, factors, preferred_element_type...]
    sub x3, other arithmetic: 2.67 us -> 5.86 us  [shards(): known = amplitudes - rest / divisor]
  transfers between devices with their start and end apart: 6 -> 6, of which waited for: 6 -> 6; matrix products, arithmetic and copies ran while one was open for 18% -> 22% of each run, Pallas kernels for 0% -> 0%
where the time goes in v5:
time: 318 us; the launch traced here: 317 us
  waiting for transfers between devices  110 us (35%)
  matrix products  63 us (20%)
  blocking collectives  56.6 us (18%)
  Pallas kernels  55.9 us (18%)
  starting transfers between devices  19.9 us (6%)
  other arithmetic  6.83 us (2%)
  local copies, waits for them, and re-layouts  4.44 us (1%)
    all_to_all x3, waiting for transfers between devices, swap(): lax.all_to_all(values, 'pairs', split_axis=0, concat_axis=0, tiled=True,...  106 us
    dot_general x15, matrix products, add_group(): jnp.einsum('rqad,rqbd->rab', ladder_half, factors, preferred_element_type...  63 us
    all_to_all x3, blocking collectives, swap(): lax.all_to_all(values, 'pairs', split_axis=0, concat_axis=0, tiled=True,...  56.6 us
    pallas_call x3, Pallas kernels, pick_pieces(): pl.pallas_call(pick_kernel, grid_spec=pltpu.PrefetchScalarGridSpec(num_sc...  29.3 us
    pallas_call x3, Pallas kernels, couple(): pl.pallas_call(functools.partial(couple_kernel, first, last), in_specs=[s...  23.9 us
    all_to_all x3, starting transfers between devices, swap(): lax.all_to_all(values, 'pairs', split_axis=0, concat_axis=0, tiled=True,...  12.8 us
    ppermute x3, starting transfers between devices, shards(): mate = lax.ppermute(near, 'pairs', mates)  7.03 us
  transfers between devices with their start and end apart: 6, of which 6 were waited for; matrix products, arithmetic and copies ran while one was open for 22% of the time, Pallas kernels for 0%

profile of v5, /device:TPU:1, one launch (start us, length us, event | category | flops | bytes accessed | tf_op | source)
XLA Modules:
  0.0 317.2 jit_solution(4681617276500961014)
XLA Ops:
  2.7 26.5 %all_to_all.30 = bf16[64,8,768]{2,1,0:T(8,128)(2,1)S(1)} all-to-all(bf16[64,8,768]{2,1,0:T(8,128)(2,1)} %get-tuple-element.253), channel_id=1, replica_groups={{0,2,4,6,8,10,12,14,16,18,20,22,24,26,28,30,32,34,36,38,40,42,44,46,48,..., dimensions={0} | all-to-all | bytes 1572864 | tf_op jit(solution)/shard_map/all_to_all | solution.py:279
  34.9 14.3 %pick_pieces.3 = bf16[64,2,48,640]{3,2,1,0:T(8,128)(2,1)} custom-call(s32[1]{0:T(128)} %bitcast.core_ref, s32[4,48,32]{2,1,0:T(8,128)} %bitcast.85, bf16[512,768]{1,0:T(8,128)(2,1)} %bitcast.80, bf16[512,768]{1,0:T(8,128)(2,1)} %bitcast.88), custom_call_target="tpu_custom_call" | custom-call | flops 8053063680 | bytes 9175040 | tf_op jit(solution)/shard_map/pick_pieces/pallas_call | solution.py:132
  49.2 5.1 %all-to-all-start.1 = ((bf16[128,48,640]{2,1,0:T(8,128)(2,1)}), bf16[128,48,640]{2,1,0:T(8,128)(2,1)}, u32[]{:S(2)}, u32[]{:S(2)}) async-start(bf16[128,48,640]{2,1,0:T(8,128)(2,1)} %bitcast.77), calls=%async_computation.1 | async-start | bytes 15728640 | tf_op jit(solution)/shard_map/all_to_all | solution.py:279
  55.0 18.5 %while.42 = (s32[]{:T(128)}, f32[8,128,128]{2,1,0:T(8,128)S(1)}, bf16[8,40,128,128]{3,2,1,0:T(8,128)(2,1)}, bf16[8,128,128]{2,1,0:T(8,128)(2,1)S(1)}, s32[]{:T(128)}, /*index=5*/s32[]{:T(128)}, s32[]{:T(128)}, s32[]{:T(128)}) while((s32[]{:T(128)}, f32[8,128,128]{2,1,0:T(8,128)S(1)}, bf16[8,40,128,128]{3,2,1,0:T(8,128)(2,1)}, ...), condition=%wide.region_1.2_spmd.clone, body=%wide.region_0.1_spmd.clone.sunk | while | flops 538181632 | bytes 5506700 | solution.py:327
  74.7 71.8 %all-to-all-done.1 = bf16[128,48,640]{2,1,0:T(8,128)(2,1)} async-done(((bf16[128,48,640]{2,1,0:T(8,128)(2,1)}), bf16[128,48,640]{2,1,0:T(8,128)(2,1)}, u32[]{:S(2)}, u32[]{:S(2)}) %all-to-all-start.1) | async-done | bytes 7864352 | tf_op jit(solution)/shard_map/all_to_all | solution.py:279
  146.5 10.8 %couple.3 = (f32[8,128,128]{2,1,0:T(8,128)}, bf16[8,128,128]{2,1,0:T(8,128)(2,1)}, bf16[64,8,256]{2,1,0:T(8,128)(2,1)}, bf16[8,128,1536]{2,1,0:T(8,128)(2,1)}) custom-call(f32[8,12]{1,0:T(8,128)} %convert_element_type.42.refs_0_, f32[8]{0:T(128)} %refs_1_.5, f32[8,128]{1,0:T(8,128)} %refs_2_.5, ...), custom_call_target="tpu_custom_call", output_to_operand_aliasing={{0}: (5, {})} | custom-call | tf_op jit(solution)/shard_map/couple/pallas_call | solution.py:266
  157.3 16.9 %all_to_all.31 = bf16[64,8,256]{2,1,0:T(8,128)(2,1)S(1)} all-to-all(bf16[64,8,256]{2,1,0:T(8,128)(2,1)} %get-tuple-element.258), channel_id=1, replica_groups={{0,2,4,6,8,10,12,14,16,18,20,22,24,26,28,30,32,34,36,38,40,42,44,46,48,..., dimensions={0} | all-to-all | bytes 524288 | tf_op jit(solution)/shard_map/all_to_all | solution.py:279
  178.3 7.5 %pick_pieces.4 = bf16[64,2,48,256]{3,2,1,0:T(8,128)(2,1)} custom-call(s32[1]{0:T(128)} %bitcast.core_ref, s32[4,48,32]{2,1,0:T(8,128)} %bitcast.86, bf16[512,256]{1,0:T(8,128)(2,1)} %bitcast.82, bf16[512,256]{1,0:T(8,128)(2,1)} %bitcast.90), custom_call_target="tpu_custom_call" | custom-call | flops 3221225472 | bytes 3670016 | tf_op jit(solution)/shard_map/pick_pieces/pallas_call | solution.py:132
  189.7 22.4 %while.43 = (s32[]{:T(128)}, f32[8,128,128]{2,1,0:T(8,128)}, bf16[8,40,128,128]{3,2,1,0:T(8,128)(2,1)}, bf16[8,128,128]{2,1,0:T(8,128)(2,1)}, s32[]{:T(128)}, /*index=5*/s32[]{:T(128)}, s32[]{:T(128)}, s32[]{:T(128)}) while((s32[]{:T(128)}, f32[8,128,128]{2,1,0:T(8,128)}, bf16[8,40,128,128]{3,2,1,0:T(8,128)(2,1)}, ...), condition=%wide.region_3.4_spmd.clone, body=%wide.region_2.3_spmd.clone.sunk | while | flops 538181632 | bytes 5506700 | solution.py:327
  194.2 4.5 %fusion.108 = f32[8,128,128]{2,1,0:T(8,128)} fusion(bf16[8,40,128,128]{3,2,1,0:T(8,128)(2,1)} %get-tuple-element.455, s32[]{:T(128)S(6)} %select_n.78, f32[8,128,128]{2,1,0:T(8,128)} %get-tuple-element.446, bf16[8,128,128]{2,1,0:T(8,128)(2,1)} %get-tuple-element.456, pred[]{:T(512)S(6)} %compare.16), kind=kOutput, calls=%fused_computation.13.clone.1 | convolution fusion | flops 538181632 | bytes 5506560 | tf_op jit(solution)/shard_map/while/body/eval_jaxpr/rqad,rqbd->rab/dot_general | solution.py:323
  198.7 4.5 %fusion.108 = f32[8,128,128]{2,1,0:T(8,128)} fusion(bf16[8,40,128,128]{3,2,1,0:T(8,128)(2,1)} %get-tuple-element.455, s32[]{:T(128)S(6)} %select_n.78, f32[8,128,128]{2,1,0:T(8,128)} %get-tuple-element.446, bf16[8,128,128]{2,1,0:T(8,128)(2,1)} %get-tuple-element.456, pred[]{:T(512)S(6)} %compare.16), kind=kOutput, calls=%fused_computation.13.clone.1 | convolution fusion | flops 538181632 | bytes 5506560 | tf_op jit(solution)/shard_map/while/body/eval_jaxpr/rqad,rqbd->rab/dot_general | solution.py:323
  203.2 4.5 %fusion.108 = f32[8,128,128]{2,1,0:T(8,128)} fusion(bf16[8,40,128,128]{3,2,1,0:T(8,128)(2,1)} %get-tuple-element.455, s32[]{:T(128)S(6)} %select_n.78, f32[8,128,128]{2,1,0:T(8,128)} %get-tuple-element.446, bf16[8,128,128]{2,1,0:T(8,128)(2,1)} %get-tuple-element.456, pred[]{:T(512)S(6)} %compare.16), kind=kOutput, calls=%fused_computation.13.clone.1 | convolution fusion | flops 538181632 | bytes 5506560 | tf_op jit(solution)/shard_map/while/body/eval_jaxpr/rqad,rqbd->rab/dot_general | solution.py:323
  207.6 4.4 %fusion.108 = f32[8,128,128]{2,1,0:T(8,128)} fusion(bf16[8,40,128,128]{3,2,1,0:T(8,128)(2,1)} %get-tuple-element.455, s32[]{:T(128)S(6)} %select_n.78, f32[8,128,128]{2,1,0:T(8,128)} %get-tuple-element.446, bf16[8,128,128]{2,1,0:T(8,128)(2,1)} %get-tuple-element.456, pred[]{:T(512)S(6)} %compare.16), kind=kOutput, calls=%fused_computation.13.clone.1 | convolution fusion | flops 538181632 | bytes 5506560 | tf_op jit(solution)/shard_map/while/body/eval_jaxpr/rqad,rqbd->rab/dot_general | solution.py:323
  214.4 17.0 %all-to-all-done.3 = bf16[128,48,256]{2,1,0:T(8,128)(2,1)S(1)} async-done(((bf16[128,48,256]{2,1,0:T(8,128)(2,1)}), bf16[128,48,256]{2,1,0:T(8,128)(2,1)S(1)}, u32[]{:S(2)}, u32[]{:S(2)}) %all-to-all-start.3) | async-done | bytes 3145760 | tf_op jit(solution)/shard_map/all_to_all | solution.py:279
  232.5 7.9 %couple.4 = (f32[8,128,128]{2,1,0:T(8,128)S(1)}, bf16[8,128,128]{2,1,0:T(8,128)(2,1)}, bf16[64,8,256]{2,1,0:T(8,128)(2,1)S(1)}) custom-call(f32[8,12]{1,0:T(8,128)S(1)} %copy-done.4, f32[8]{0:T(128)S(1)} %copy-done.6, f32[8,128]{1,0:T(8,128)S(1)} %copy-done.3, bf16[64,2,6,8,256]{4,3,2,1,0:T(8,128)(2,1)S(1)} %bitcast.76, ...), custom_call_target="tpu_custom_call", output_to_operand_aliasing={{0}: (5, {})} | custom-call | tf_op jit(solution)/shard_map/couple/pallas_call | solution.py:266
  241.2 13.2 %all_to_all.32 = bf16[64,8,256]{2,1,0:T(8,128)(2,1)S(1)} all-to-all(bf16[64,8,256]{2,1,0:T(8,128)(2,1)S(1)} %get-tuple-element.263), channel_id=1, replica_groups={{0,2,4,6,8,10,12,14,16,18,20,22,24,26,28,30,32,34,36,38,40,42,44,46,48,..., dimensions={0} | all-to-all | bytes 524288 | tf_op jit(solution)/shard_map/all_to_all | solution.py:279
  258.7 7.5 %pick_pieces.5 = bf16[64,2,48,256]{3,2,1,0:T(8,128)(2,1)} custom-call(s32[1]{0:T(128)} %bitcast.core_ref, s32[4,48,32]{2,1,0:T(8,128)} %bitcast.87, bf16[512,256]{1,0:T(8,128)(2,1)} %bitcast.81, bf16[512,256]{1,0:T(8,128)(2,1)} %bitcast.89), custom_call_target="tpu_custom_call" | custom-call | flops 3221225472 | bytes 3670016 | tf_op jit(solution)/shard_map/pick_pieces/pallas_call | solution.py:132
  270.0 22.3 %while.44 = (s32[]{:T(128)}, f32[8,128,128]{2,1,0:T(8,128)}, bf16[8,40,128,128]{3,2,1,0:T(8,128)(2,1)}, bf16[8,128,128]{2,1,0:T(8,128)(2,1)}, s32[]{:T(128)}, /*index=5*/s32[]{:T(128)}, s32[]{:T(128)}, s32[]{:T(128)}) while((s32[]{:T(128)}, f32[8,128,128]{2,1,0:T(8,128)}, bf16[8,40,128,128]{3,2,1,0:T(8,128)(2,1)}, ...), condition=%wide.region_5.6_spmd.clone, body=%wide.region_4.5_spmd.clone.sunk | while | flops 538181632 | bytes 5506700 | solution.py:327
  274.5 4.5 %fusion.113 = f32[8,128,128]{2,1,0:T(8,128)} fusion(bf16[8,40,128,128]{3,2,1,0:T(8,128)(2,1)} %get-tuple-element.479, s32[]{:T(128)S(6)} %select_n.79, f32[8,128,128]{2,1,0:T(8,128)} %get-tuple-element.470, bf16[8,128,128]{2,1,0:T(8,128)(2,1)} %get-tuple-element.480, pred[]{:T(512)S(6)} %compare.17), kind=kOutput, calls=%fused_computation.21.clone.1 | convolution fusion | flops 538181632 | bytes 5506560 | tf_op jit(solution)/shard_map/while/body/eval_jaxpr/rqad,rqbd->rab/dot_general | solution.py:323
  279.0 4.4 %fusion.113 = f32[8,128,128]{2,1,0:T(8,128)} fusion(bf16[8,40,128,128]{3,2,1,0:T(8,128)(2,1)} %get-tuple-element.479, s32[]{:T(128)S(6)} %select_n.79, f32[8,128,128]{2,1,0:T(8,128)} %get-tuple-element.470, bf16[8,128,128]{2,1,0:T(8,128)(2,1)} %get-tuple-element.480, pred[]{:T(512)S(6)} %compare.17), kind=kOutput, calls=%fused_computation.21.clone.1 | convolution fusion | flops 538181632 | bytes 5506560 | tf_op jit(solution)/shard_map/while/body/eval_jaxpr/rqad,rqbd->rab/dot_general | solution.py:323
  283.5 4.5 %fusion.113 = f32[8,128,128]{2,1,0:T(8,128)} fusion(bf16[8,40,128,128]{3,2,1,0:T(8,128)(2,1)} %get-tuple-element.479, s32[]{:T(128)S(6)} %select_n.79, f32[8,128,128]{2,1,0:T(8,128)} %get-tuple-element.470, bf16[8,128,128]{2,1,0:T(8,128)(2,1)} %get-tuple-element.480, pred[]{:T(512)S(6)} %compare.17), kind=kOutput, calls=%fused_computation.21.clone.1 | convolution fusion | flops 538181632 | bytes 5506560 | tf_op jit(solution)/shard_map/while/body/eval_jaxpr/rqad,rqbd->rab/dot_general | solution.py:323
  287.9 4.4 %fusion.113 = f32[8,128,128]{2,1,0:T(8,128)} fusion(bf16[8,40,128,128]{3,2,1,0:T(8,128)(2,1)} %get-tuple-element.479, s32[]{:T(128)S(6)} %select_n.79, f32[8,128,128]{2,1,0:T(8,128)} %get-tuple-element.470, bf16[8,128,128]{2,1,0:T(8,128)(2,1)} %get-tuple-element.480, pred[]{:T(512)S(6)} %compare.17), kind=kOutput, calls=%fused_computation.21.clone.1 | convolution fusion | flops 538181632 | bytes 5506560 | tf_op jit(solution)/shard_map/while/body/eval_jaxpr/rqad,rqbd->rab/dot_general | solution.py:323
  294.7 17.1 %all-to-all-done.5 = bf16[128,48,256]{2,1,0:T(8,128)(2,1)S(1)} async-done(((bf16[128,48,256]{2,1,0:T(8,128)(2,1)}), bf16[128,48,256]{2,1,0:T(8,128)(2,1)S(1)}, u32[]{:S(2)}, u32[]{:S(2)}) %all-to-all-start.5) | async-done | bytes 3145760 | tf_op jit(solution)/shard_map/all_to_all | solution.py:279
  311.8 5.2 %couple.5 = f32[8,128,128]{2,1,0:T(8,128)} custom-call(f32[8,12]{1,0:T(8,128)S(1)} %copy-done.4, f32[8]{0:T(128)S(1)} %copy-done.6, f32[8,128]{1,0:T(8,128)S(1)} %copy-done.3, bf16[64,2,6,8,256]{4,3,2,1,0:T(8,128)(2,1)S(1)} %bitcast.75, bf16[8,128,1536]{2,1,0:T(8,128)(2,1)} %get-tuple-element.259.refs_4_, ...), custom_call_target="tpu_custom_call", output_to_operand_aliasing={{}: (5, {})} | custom-call | tf_op jit(solution)/shard_map/couple/pallas_call | solution.py:266
  (69 shorter events, 60.0 us)
Async XLA Ops:
  29.3 5.6 %copy-start.8 = (bf16[64,8,768]{2,1,0:T(8,128)(2,1)}, bf16[64,8,768]{2,1,0:T(8,128)(2,1)S(1)}, u32[]{:S(2)}) copy-start(bf16[64,8,768]{2,1,0:T(8,128)(2,1)S(1)} %all_to_all.30) | copy-start | bytes 2359300
  29.3 4.3 %collective-permute-start = (bf16[64,8,768]{2,1,0:T(8,128)(2,1)S(1)}, bf16[64,8,768]{2,1,0:T(8,128)(2,1)S(1)}, u32[]{:S(2)}, u32[]{:S(2)}) collective-permute-start(bf16[64,8,768]{2,1,0:T(8,128)(2,1)S(1)} %all_to_all.30), channel_id=1, source_target_pairs={{0,1},{1,0},{2,3},{3,2},{4,5},{5,4},{6,7},{7,6},{8,9},{9,8},{10,11... | collective-permute-start | bytes 2359304 | tf_op jit(solution)/shard_map/ppermute | solution.py:338
  33.5 1.4 copy-start.12
  49.2 5.1 %copy-start.13 = (bf16[8,12]{1,0:T(8,128)(2,1)S(1)}, bf16[8,12]{1,0:T(8,128)(2,1)}, u32[]{:S(2)}) copy-start(bf16[8,12]{1,0:T(8,128)(2,1)} %param.23) | copy-start | bytes 580
  49.2 5.7 %copy-start.14 = (s32[8]{0:T(128)S(1)}, s32[8]{0:T(128)}, u32[]{:S(2)}) copy-start(s32[8]{0:T(128)} %count_ref.1) | copy-start | bytes 100
  49.2 97.3 %all-to-all-start.1 = ((bf16[128,48,640]{2,1,0:T(8,128)(2,1)}), bf16[128,48,640]{2,1,0:T(8,128)(2,1)}, u32[]{:S(2)}, u32[]{:S(2)}) async-start(bf16[128,48,640]{2,1,0:T(8,128)(2,1)} %bitcast.77), calls=%async_computation.1 | async-start | bytes 15728640 | tf_op jit(solution)/shard_map/all_to_all | solution.py:279
  55.0 18.5 %copy-start.2 = (f32[8,128]{1,0:T(8,128)S(1)}, f32[8,128]{1,0:T(8,128)}, u32[]{:S(2)}) copy-start(f32[8,128]{1,0:T(8,128)} %refs_2_.5) | copy-start | bytes 12292
  55.0 18.5 %copy-start.5 = (f32[8]{0:T(128)S(1)}, f32[8]{0:T(128)}, u32[]{:S(2)}) copy-start(f32[8]{0:T(128)} %refs_1_.5) | copy-start | bytes 100
  55.0 18.5 %copy-start.7 = (bf16[8,128,128]{2,1,0:T(8,128)(2,1)S(1)}, bf16[8,128,128]{2,1,0:T(8,128)(2,1)}, u32[]{:S(2)}) copy-start(bf16[8,128,128]{2,1,0:T(8,128)(2,1)} %exchange_ref.1) | copy-start | bytes 786436
  55.0 18.5 %copy-start.9 = (f32[8,128,128]{2,1,0:T(8,128)S(1)}, f32[8,128,128]{2,1,0:T(8,128)}, u32[]{:S(2)}) copy-start(f32[8,128,128]{2,1,0:T(8,128)} %get-tuple-element.255) | copy-start | bytes 1572868
  174.1 3.5 %copy-start.11 = (bf16[64,8,256]{2,1,0:T(8,128)(2,1)}, bf16[64,8,256]{2,1,0:T(8,128)(2,1)S(1)}, u32[]{:S(2)}) copy-start(bf16[64,8,256]{2,1,0:T(8,128)(2,1)S(1)} %all_to_all.31) | copy-start | bytes 786436
  174.1 3.5 %collective-permute-start.1 = (bf16[64,8,256]{2,1,0:T(8,128)(2,1)S(1)}, bf16[64,8,256]{2,1,0:T(8,128)(2,1)S(1)}, u32[]{:S(2)}, u32[]{:S(2)}) collective-permute-start(bf16[64,8,256]{2,1,0:T(8,128)(2,1)S(1)} %all_to_all.31), channel_id=1, source_target_pairs={{0,1},{1,0},{2,3},{3,2},{4,5},{5,4},{6,7},{7,6},{8,9},{9,8},{10,11... | collective-permute-start | bytes 786440 | tf_op jit(solution)/shard_map/ppermute | solution.py:338
  177.6 0.7 copy-start.16
  185.8 45.6 %all-to-all-start.3 = ((bf16[128,48,256]{2,1,0:T(8,128)(2,1)}), bf16[128,48,256]{2,1,0:T(8,128)(2,1)S(1)}, u32[]{:S(2)}, u32[]{:S(2)}) async-start(bf16[128,48,256]{2,1,0:T(8,128)(2,1)} %bitcast.79), calls=%async_computation.3 | async-start | bytes 6291456 | tf_op jit(solution)/shard_map/all_to_all | solution.py:279
  189.7 22.4 %copy-start.3 = (f32[8,128]{1,0:T(8,128)S(1)}, f32[8,128]{1,0:T(8,128)}, u32[]{:S(2)}) copy-start(f32[8,128]{1,0:T(8,128)} %refs_2_.5) | copy-start | bytes 12292
  189.7 22.4 %copy-start.6 = (f32[8]{0:T(128)S(1)}, f32[8]{0:T(128)}, u32[]{:S(2)}) copy-start(f32[8]{0:T(128)} %refs_1_.5) | copy-start | bytes 100
  189.7 41.7 %copy-start.4 = (f32[8,12]{1,0:T(8,128)S(1)}, f32[8,12]{1,0:T(8,128)}, u32[]{:S(2)}) copy-start(f32[8,12]{1,0:T(8,128)} %convert_element_type.42.refs_0_) | copy-start | bytes 1156
  231.4 1.0 copy-start
  240.4 0.8 copy-start.1
  254.5 3.5 %copy-start.10 = (bf16[64,8,256]{2,1,0:T(8,128)(2,1)}, bf16[64,8,256]{2,1,0:T(8,128)(2,1)S(1)}, u32[]{:S(2)}) copy-start(bf16[64,8,256]{2,1,0:T(8,128)(2,1)S(1)} %all_to_all.32) | copy-start | bytes 786436
  254.5 3.5 %collective-permute-start.2 = (bf16[64,8,256]{2,1,0:T(8,128)(2,1)S(1)}, bf16[64,8,256]{2,1,0:T(8,128)(2,1)S(1)}, u32[]{:S(2)}, u32[]{:S(2)}) collective-permute-start(bf16[64,8,256]{2,1,0:T(8,128)(2,1)S(1)} %all_to_all.32), channel_id=1, source_target_pairs={{0,1},{1,0},{2,3},{3,2},{4,5},{5,4},{6,7},{7,6},{8,9},{9,8},{10,11... | collective-permute-start | bytes 786440 | tf_op jit(solution)/shard_map/ppermute | solution.py:338
  258.0 0.7 copy-start.15
  266.2 45.6 %all-to-all-start.5 = ((bf16[128,48,256]{2,1,0:T(8,128)(2,1)}), bf16[128,48,256]{2,1,0:T(8,128)(2,1)S(1)}, u32[]{:S(2)}, u32[]{:S(2)}) async-start(bf16[128,48,256]{2,1,0:T(8,128)(2,1)} %bitcast.78), calls=%async_computation.5 | async-start | bytes 6291456 | tf_op jit(solution)/shard_map/all_to_all | solution.py:279
